TPU v7x, 128 devices: a whole 4x4x4 slice. The times are simulated.
128 devices in a mesh: row: 8 (over z_lo, y), col: 16 (over z_hi, x, core).
Axes of the slice: x: 4, y: 4, z: 4 (z_hi: 2, z_lo: 2; z = z_hi * 2 + z_lo), core: 2. Of those that a mesh axis runs over, the one named last changes fastest.
Arguments:
- front: float32 [16384, 16384], P('row', 'col'), as said below
- child_updates: bfloat16 [8, 4096, 4096], P('row', 'col'), as said below
- child_maps: int32 [8, 16], replicated, may hold values from 0 to 63, as said below
- fill_mask: int32 [64, 64], replicated, may hold values from 0 to 1, as said below
Outputs:
- factored: float32 [16384, 16384], P('row', 'col')
Inputs may be any that keep to these rules, and one draw needn't show every extreme that they name: front is symmetric. `child_updates`: each child's matrix is symmetric. `child_maps`: each row lists 16 distinct block indices in ascending order; in every aligned run of 4 indices a row names at most 2, and exactly 2 in some run; in every aligned run of 8 indices at most 4, and exactly 4 in some run. `fill_mask`: symmetric, ones on the diagonal.
All inputs are finite; a program needn't handle non-finite values.
Results may differ from a plain program's by a relative error of at most 0.0003.
Values may be sent and summed in bfloat16 or wider, within the bound.
A program may use at most 192 MiB of HBM per device.

v0:
```python
import jax
import jax.numpy as jnp
from jax import lax
from jax.sharding import PartitionSpec as P

BS = 256
CB = 16
PB = 2
STEPS = 2


def broadcast(shard, axis, root):
    mine = lax.axis_index(axis) == root
    return lax.psum(jnp.where(mine, shard, jnp.zeros_like(shard)), axis)


def span_ranks(spans):
    items_count = spans.shape[-1]
    agrees = spans[..., :, None] == spans[..., None, :]
    earlier = jnp.arange(items_count)[None, :] < jnp.arange(items_count)[:, None]
    return jnp.sum(agrees & earlier, axis=-1)


def one_hot_slots(spans, ranks, slot_groups, slot_depth):
    matches = (spans[None, None, :] == jnp.arange(slot_groups)[:, None, None]) & (
        ranks[None, None, :] == jnp.arange(slot_depth)[None, :, None]
    )
    return matches.astype(jnp.bfloat16)


def placement(block_map, span_index, per_span, slot_depth):
    spans = block_map // per_span
    ranks = span_ranks(spans)
    local_block = block_map - span_index * per_span
    matches = (
        (spans[:, None, None, :] == span_index)
        & (ranks[:, None, None, :] == jnp.arange(slot_depth)[None, None, :, None])
        & (local_block[:, None, None, :] == jnp.arange(per_span)[None, :, None, None])
    )
    return jnp.sum(matches.astype(jnp.int32), axis=-1).astype(jnp.bfloat16)


def triangular(factor, panel_rows):
    return jax.scipy.linalg.solve_triangular(factor, panel_rows.T, lower=True).T


def pivot_of(panel_rows, row_owner, row_at, panel_width):
    return broadcast(panel_rows[row_at : row_at + panel_width], "row", row_owner)


def local(front, child_updates, child_maps, fill_mask):
    row_len, col_len = front.shape
    n_row = lax.axis_size("row")
    n_col = lax.axis_size("col")
    row_me = lax.axis_index("row")
    col_me = lax.axis_index("col")
    edge_len = BS
    row_blocks = row_len // edge_len
    col_blocks = col_len // edge_len
    depth_col = 2
    depth_row = 2 * (n_col // n_row)
    panel_width = PB * BS
    own_map = lax.dynamic_index_in_dim(child_maps, row_me, 0, keepdims=False)
    col_spans = own_map // col_blocks
    pack_cols = one_hot_slots(col_spans, span_ranks(col_spans), n_col, depth_col)
    updates = child_updates[0]
    local_rows = updates.shape[0]
    tiles_grid = updates.reshape(local_rows, CB, edge_len)
    packed = jnp.einsum(
        "jtb,xby->jxty", pack_cols, tiles_grid, preferred_element_type=jnp.float32
    ).astype(jnp.bfloat16)
    packed = packed.reshape(n_col, local_rows, depth_col * edge_len)
    gathered = lax.all_to_all(packed, "col", split_axis=0, concat_axis=0, tiled=True)
    row_spans = own_map // row_blocks
    pack_rows = one_hot_slots(row_spans, span_ranks(row_spans), n_row, depth_row)
    packed_two = jnp.einsum(
        "rsa,axz->rsxz", pack_rows, gathered, preferred_element_type=jnp.float32
    ).astype(jnp.bfloat16)
    packed_two = packed_two.reshape(n_row, depth_row * edge_len, depth_col * edge_len)
    arrived = lax.all_to_all(packed_two, "row", split_axis=0, concat_axis=0, tiled=True)
    arrived = arrived.reshape(n_row, depth_row, edge_len, depth_col * edge_len)
    rows_place = placement(child_maps, row_me, row_blocks, depth_row)
    cols_place = placement(child_maps, col_me, col_blocks, depth_col)
    placed = jnp.einsum(
        "kis,ksxz->kixz", rows_place, arrived, preferred_element_type=jnp.float32
    ).astype(jnp.bfloat16)
    placed = placed.reshape(n_row, row_blocks, edge_len, depth_col, edge_len)
    assembled = jnp.einsum(
        "kixty,kjt->ixjy", placed, cols_place, preferred_element_type=jnp.float32
    )
    mask_local = lax.dynamic_slice(
        fill_mask, (row_me * row_blocks, col_me * col_blocks), (row_blocks, col_blocks)
    ).astype(jnp.float32)
    mask_full = jnp.broadcast_to(
        mask_local[:, None, :, None], (row_blocks, edge_len, col_blocks, edge_len)
    ).reshape(row_len, col_len)
    working = (front + assembled.reshape(row_len, col_len)) * mask_full
    global_rows = row_me * row_len + jnp.arange(row_len)
    global_cols = col_me * col_len + jnp.arange(col_len)
    lower_blocks = global_rows[:, None] // edge_len >= global_cols[None, :] // edge_len
    source_row = col_me * col_len // row_len
    source_offset = col_me * col_len % row_len
    for step_index in range(STEPS):
        first_col = step_index * panel_width
        finish = first_col + panel_width
        col_owner = first_col // col_len
        col_at = first_col % col_len
        row_owner = first_col // row_len
        row_at = first_col % row_len
        panel_local = working[:, col_at : col_at + panel_width]
        pivot_rows = (global_rows >= first_col) & (global_rows < finish)
        factor = jnp.linalg.cholesky(pivot_of(panel_local, row_owner, row_at, panel_width))
        factor_padded = lax.dynamic_update_slice_in_dim(
            jnp.zeros((row_len, panel_width), jnp.float32), factor, row_at, 0
        )
        solved = jnp.where(pivot_rows[:, None], factor_padded, triangular(factor, panel_local))
        rows_factor = broadcast(solved, "col", col_owner)
        picked = lax.dynamic_slice_in_dim(rows_factor, source_offset, col_len, 0)
        cols_factor = broadcast(picked.astype(jnp.bfloat16), "row", source_row).astype(picked.dtype)
        product = jnp.dot(
            rows_factor,
            cols_factor.T,
            precision=lax.Precision.HIGHEST,
            preferred_element_type=jnp.float32,
        )
        trailing = (global_cols >= finish)[None, :]
        working = jnp.where(trailing, working - product * mask_full, working)
        current = working[:, col_at : col_at + panel_width]
        panel_now = jnp.where(col_me == col_owner, rows_factor, current)
        working = lax.dynamic_update_slice_in_dim(working, panel_now, col_at, 1)
    return jnp.where(lower_blocks, working, 0.0)


def solution(mesh):
    placed = (P("row", "col"), P("row", "col", None), P(), P())
    return jax.shard_map(
        local, mesh=mesh, in_specs=placed, out_specs=P("row", "col"), check_vma=False
    )
```

profile of v0, /device:TPU:112, one launch (start us, length us, event | category | flops | bytes accessed | tf_op | source)
XLA Modules:
  0.0 1285.0 jit_solution(16817608450089591911)
XLA Ops:
  34.4 55.6 %all-to-all-done = bf16[16,256,512]{2,1,0:T(8,128)(2,1)} async-done(((bf16[16,256,512]{2,1,0:T(8,128)(2,1)}), bf16[16,256,512]{2,1,0:T(8,128)(2,1)}, u32[]{:S(2)}, u32[]{:S(2)}) %all-to-all-start) | async-done | bytes 4194336 | tf_op jit(solution)/shard_map/all_to_all | solution.py:73
  98.4 9.5 copy.92
  122.8 9.2 copy.97
  133.4 94.8 %all-to-all-done.1 = bf16[8,1024,512]{2,1,0:T(8,128)(2,1)} async-done(((bf16[8,1024,512]{2,1,0:T(8,128)(2,1)}), bf16[8,1024,512]{2,1,0:T(8,128)(2,1)}, u32[]{:S(2)}, u32[]{:S(2)}) %all-to-all-start.1) | async-done | bytes 8388640 | tf_op jit(solution)/shard_map/all_to_all | solution.py:80
  228.2 13.9 %convolution_convert_fusion = bf16[8,8,256,512]{3,1,2,0:T(8,128)(2,1)} fusion(bf16[8,4,256,512]{3,2,1,0:T(8,128)(2,1)} %bitcast.14, s32[8,8,4]{1,2,0:T(4,128)S(1)} %convert_reduce_fusion), kind=kOutput, calls=%fused_computation.8 | convolution fusion | flops 75497728 | bytes 25166848 | tf_op jit(solution)/shard_map/kis,ksxz->kixz/dot_general | solution.py:84
  242.1 30.2 %fusion = f32[4,8,256,256,1]{3,0,4,2,1:T(4,128)} fusion(bf16[8,8,256,2,256]{4,1,3,2,0:T(8,128)(2,1)} %bitcast.176, bf16[8,4,2,1,1]{0,2,1,4,3:T(2,128)(2,1)S(1)} %convert_bitcast_fusion.1), kind=kOutput, calls=%fused_computation.4 | convolution fusion | flops 67108864 | bytes 25165952 | tf_op jit(solution)/shard_map/kixty,kjt->ixjy/dot_general | solution.py:88
  290.1 9.6 add_multiply_fusion
  308.7 81.3 %all-reduce.10.cloned.1.call-done = f32[512,512]{0,1:T(8,128)} async-done(((f32[512,512]{0,1:T(8,128)}), f32[512,512]{0,1:T(8,128)}) %all-reduce.10.cloned.1.call-update) | async-done | bytes 1048592 | tf_op jit(solution)/shard_map/psum | solution.py:14
  393.0 11.7 cholesky.286
  404.8 9.8 custom-call.27
  415.2 11.7 cholesky.305
  427.3 10.2 custom-call.28
  438.6 11.7 cholesky.326
  450.5 9.8 custom-call.29
  461.1 11.9 cholesky.343
  486.7 39.3 %custom-call.30 = f32[4,128,128]{1,2,0:T(8,128)S(1)} custom-call(f32[4,128,128]{2,1,0:T(8,128)S(1)} %get-tuple-element.21), custom_call_target="InvertDiagBlocksLowerTriangular" | custom-call | tf_op jit(solution)/shard_map/jit(_solve_triangular)/triangular_solve | solution.py:44
  539.9 151.0 %all-reduce.12.cloned.1.call-done = f32[2048,512]{0,1:T(8,128)} async-done(((f32[2048,512]{0,1:T(8,128)}), f32[2048,512]{0,1:T(8,128)}) %all-reduce.12.cloned.1.call-update) | async-done | bytes 4194320 | tf_op jit(solution)/shard_map/psum | solution.py:14
  693.8 77.1 %all-reduce.14.cloned.1.call-done = bf16[1024,512]{0,1:T(8,128)(2,1)} async-done(((bf16[1024,512]{0,1:T(8,128)(2,1)}), bf16[1024,512]{0,1:T(8,128)(2,1)}) %all-reduce.14.cloned.1.call-update) | async-done | bytes 1048592 | tf_op jit(solution)/shard_map/psum | solution.py:14
  770.9 14.3 %subtract_select_fusion.1 = f32[2048,1024]{0,1:T(8,128)S(1)} fusion(f32[2048,1024]{0,1:T(8,128)} %copy-done.1, f32[2048,1024]{0,1:T(8,128)} %bitcast.174, f32[2048,512]{0,1:T(8,128)} %all-reduce.12.cloned.1.call-done, bf16[1024,512]{0,1:T(8,128)(2,1)} %all-reduce.14.cloned.1.call-done, pred[1024]{0:T(1024)(128)(4,1)S(1)} %fusion.104), kind=kOutput, calls=%fused_computation.7 | convolution fusion | flops 12891193344 | bytes 30409728 | tf_op jit(solution)/shard_map/dot_general | solution.py:120
  795.6 72.1 %all-reduce.16.cloned.1.call-done = f32[512,512]{0,1:T(8,128)} async-done(((f32[512,512]{0,1:T(8,128)}), f32[512,512]{0,1:T(8,128)}) %all-reduce.16.cloned.1.call-update) | async-done | bytes 1048592 | tf_op jit(solution)/shard_map/psum | solution.py:14
  870.7 11.7 cholesky.358
  882.5 9.8 custom-call.31
  892.9 11.7 cholesky.377
  905.0 10.0 custom-call.32
  916.1 11.7 cholesky.398
  927.9 9.8 custom-call.33
  938.6 11.9 cholesky.415
  964.9 39.3 %custom-call.34 = f32[4,128,128]{1,2,0:T(8,128)S(1)} custom-call(f32[4,128,128]{2,1,0:T(8,128)S(1)} %get-tuple-element.22), custom_call_target="InvertDiagBlocksLowerTriangular" | custom-call | tf_op jit(solution)/shard_map/jit(_solve_triangular)/triangular_solve | solution.py:44
  1018.1 151.0 %all-reduce.18.cloned.1.call-done = f32[2048,512]{0,1:T(8,128)} async-done(((f32[2048,512]{0,1:T(8,128)}), f32[2048,512]{0,1:T(8,128)}) %all-reduce.18.cloned.1.call-update) | async-done | bytes 4194320 | tf_op jit(solution)/shard_map/psum | solution.py:14
  1171.9 77.2 %all-reduce.20.cloned.1.call-done = bf16[1024,512]{0,1:T(8,128)(2,1)} async-done(((bf16[1024,512]{0,1:T(8,128)(2,1)}), bf16[1024,512]{0,1:T(8,128)(2,1)}) %all-reduce.20.cloned.1.call-update) | async-done | bytes 1048592 | tf_op jit(solution)/shard_map/psum | solution.py:14
  1249.1 14.1 %subtract_select_fusion = f32[2048,1024]{0,1:T(8,128)S(1)} fusion(f32[2048,1024]{0,1:T(8,128)} %copy-done, f32[2048,1024]{0,1:T(8,128)} %bitcast.175, f32[2048,512]{0,1:T(8,128)} %all-reduce.18.cloned.1.call-done, bf16[1024,512]{0,1:T(8,128)(2,1)} %all-reduce.20.cloned.1.call-done, pred[1024]{0:T(1024)(128)(4,1)S(1)} %fusion.103), kind=kOutput, calls=%fused_computation.6 | convolution fusion | flops 12891193344 | bytes 30409728 | tf_op jit(solution)/shard_map/dot_general | solution.py:120
  1268.4 9.2 copy.119
  (195 shorter events, 180.2 us)
Async XLA Ops:
  26.9 63.0 %all-to-all-start = ((bf16[16,256,512]{2,1,0:T(8,128)(2,1)}), bf16[16,256,512]{2,1,0:T(8,128)(2,1)}, u32[]{:S(2)}, u32[]{:S(2)}) async-start(bf16[16,256,512]{2,1,0:T(8,128)(2,1)} %copy.90), calls=%async_computation | async-start | bytes 8388608 | tf_op jit(solution)/shard_map/all_to_all | solution.py:73
  107.9 120.3 %all-to-all-start.1 = ((bf16[8,1024,512]{2,1,0:T(8,128)(2,1)}), bf16[8,1024,512]{2,1,0:T(8,128)(2,1)}, u32[]{:S(2)}, u32[]{:S(2)}) async-start(bf16[8,1024,512]{2,1,0:T(8,128)(2,1)} %copy.92), calls=%async_computation.1 | async-start | bytes 16777216 | tf_op jit(solution)/shard_map/all_to_all | solution.py:80
  113.6 276.4 %all-reduce.10.cloned.1.call-start = ((), (), s32[]{:S(2)}) async-start(), calls=%async_computation.2 | async-start | bytes 2097152 | tf_op jit(solution)/shard_map/psum | solution.py:14
  122.8 9.2 copy-start.6
  299.6 3.2 copy-start.1
  304.0 386.9 %all-reduce.12.cloned.1.call-start = ((), (), s32[]{:S(2)}) async-start(), calls=%async_computation.3 | async-start | bytes 8388608 | tf_op jit(solution)/shard_map/psum | solution.py:14
  526.0 5.8 copy-start.4
  539.8 231.1 %all-reduce.14.cloned.1.call-start = ((), (), s32[]{:S(2)}) async-start(), calls=%async_computation.4 | async-start | bytes 2097152 | tf_op jit(solution)/shard_map/psum | solution.py:14
  693.7 174.0 %all-reduce.16.cloned.1.call-start = ((), (), s32[]{:S(2)}) async-start(), calls=%async_computation.5 | async-start | bytes 2097152 | tf_op jit(solution)/shard_map/psum | solution.py:14
  770.9 14.3 %copy-start.2 = (f32[2048,512]{0,1:T(8,128)S(1)}, f32[2048,512]{0,1:T(8,128)}, u32[]{:S(2)}) copy-start(f32[2048,512]{0,1:T(8,128)} %all-reduce.12.cloned.1.call-done) | copy-start | bytes 12582916
  786.5 3.2 copy-start
  790.8 378.2 %all-reduce.18.cloned.1.call-start = ((), (), s32[]{:S(2)}) async-start(), calls=%async_computation.6 | async-start | bytes 8388608 | tf_op jit(solution)/shard_map/psum | solution.py:14
  1004.2 5.8 copy-start.5
  1018.0 231.1 %all-reduce.20.cloned.1.call-start = ((), (), s32[]{:S(2)}) async-start(), calls=%async_computation.7 | async-start | bytes 2097152 | tf_op jit(solution)/shard_map/psum | solution.py:14
  1249.1 14.1 %copy-start.3 = (f32[2048,512]{0,1:T(8,128)S(1)}, f32[2048,512]{0,1:T(8,128)}, u32[]{:S(2)}) copy-start(f32[2048,512]{0,1:T(8,128)} %all-reduce.18.cloned.1.call-done) | copy-start | bytes 12582916
Sparse Core Ops, SparseCore 0:
  304.1 85.8 all-reduce.9
  539.9 150.8 all-reduce.11
  693.8 77.0 all-reduce.13
  791.0 76.6 all-reduce.15
  1018.1 150.8 all-reduce.17
  1172.0 77.0 all-reduce.19
where the time goes:
time: 1300 us; the launch traced here: 1280 us
  waiting for transfers between devices  760 us (58%)
  other arithmetic  273 us (21%)
  matrix products  111 us (9%)
  local copies, waits for them, and re-layouts  107 us (8%)
  between operations  19.9 us (2%)
  starting transfers between devices  13.4 us (1%)
    psum x6, waiting for transfers between devices, broadcast(): return lax.psum(jnp.where(mine, shard, jnp.zeros_like(shard)), axis)  610 us
    another operation x29, other arithmetic, local(): jnp.linalg.cholesky(pivot_of(panel_local, row_owner, row_at, panel_width))  159 us
    all_to_all x1, waiting for transfers between devices, local(): lax.all_to_all(packed_two, 'row', split_axis=0, concat_axis=0, tiled=True)  94.8 us
    another operation x5, other arithmetic, triangular(): return jax.scipy.linalg.solve_triangular(factor, panel_rows.T, lower=True).T  79.1 us
    all_to_all x1, waiting for transfers between devices, local(): lax.all_to_all(packed, 'col', split_axis=0, concat_axis=0, tiled=True)  55.6 us
    unnamed x18, local copies, waits for them, and re-layouts  34 us
    dot_general x1, matrix products, local(): jnp.einsum('kixty,kjt->ixjy', placed, cols_place, preferred_element_type=...  30.2 us
    dot_general x2, matrix products, local(): jnp.dot(rows_factor, cols_factor.T, precision=lax.Precision.HIGHEST, pref...  28.4 us
  transfers between devices with their start and end apart: 8, of which 8 were waited for; matrix products, arithmetic and copies ran while one was open for 2% of the time, Pallas kernels for 0%

commit v1 on v0

v1 whole, which is shorter than its diff:
```python
import functools

import jax
import jax.numpy as jnp
from jax import lax
from jax.experimental import pallas as pl
from jax.experimental.pallas import tpu as pltpu
from jax.sharding import PartitionSpec as P

BS = 256
NR = 8
NC = 16
MESH = pl.DeviceIdType.MESH
HI = lax.Precision.HIGHEST
f32 = jnp.float32
bf16 = jnp.bfloat16
ANY = pl.BlockSpec(memory_space=pl.ANY)
VM = pl.BlockSpec(memory_space=pltpu.VMEM)
SM = pl.BlockSpec(memory_space=pltpu.SMEM)


def dot(a, b, precision=HI):
    return lax.dot_general(
        a, b, (((1,), (0,)), ((), ())), precision=precision, preferred_element_type=f32
    )


def dot_t(a, b, precision=HI):
    return lax.dot_general(
        a, b, (((1,), (1,)), ((), ())), precision=precision, preferred_element_type=f32
    )


def t_dot(a, b, precision=HI):
    return lax.dot_general(
        a, b, (((0,), (0,)), ((), ())), precision=precision, preferred_element_type=f32
    )


def row_of(x, k):
    return jnp.broadcast_to(x[k : k + 1, :], (8, 128))


def lane_of(x, k):
    return jnp.broadcast_to(x[:, k : k + 1], (8, 128))


def factor_128(m_ref, ahead=3):
    sub = lax.broadcasted_iota(jnp.int32, (8, 128), 0)
    lane = lax.broadcasted_iota(jnp.int32, (8, 128), 1)
    held = {}
    for s in range(16):
        last = min(s + ahead + 1, 16)
        for q in range(s, last):
            if q not in held:
                held[q] = (m_ref[8 * q : 8 * q + 8, :128], m_ref[8 * q : 8 * q + 8, 128:])
        left, right = held.pop(s)
        v = [lane_of(left, 8 * s + j) for j in range(8)]
        z = [jnp.where(sub == j, 1.0, 0.0).astype(f32) for j in range(8)]
        scale = jnp.zeros((8, 128), f32)
        rows, inverses = [], []
        for k in range(8):
            root = lax.rsqrt(row_of(v[k], k))
            scale = jnp.where(sub == k, root, scale)
            inverse = root * root
            inverses.append(inverse)
            below = jnp.where(sub > k, v[k], 0.0) * inverse
            row = {}
            for j in range(k + 1, 8):
                row[j] = row_of(v[j], k)
                v[j] = v[j] - below * row[j]
            rows.append(row)
            if k < 7:
                for j in range(k + 1):
                    z[j] = z[j] - below * row_of(z[j], k)
        new_left = z[0] * row_of(left, 0)
        new_right = z[0] * row_of(right, 0)
        for j in range(1, 8):
            new_left = new_left + z[j] * row_of(left, j)
            new_right = new_right + z[j] * row_of(right, j)
        new_left = jnp.where(lane >= 8 * s + sub, new_left, 0.0)
        rows_left = [row_of(new_left, k) for k in range(8)]
        rows_right = [row_of(new_right, k) for k in range(8)]
        for q in range(s + 1, last):
            x, y = held[q]
            w = [lane_of(x, 8 * s + j) for j in range(8)]
            for k in range(8):
                times = w[k] * inverses[k]
                for j in range(k + 1, 8):
                    w[j] = w[j] - times * rows[k][j]
                x = x - times * rows_left[k]
                y = y - times * rows_right[k]
            held[q] = (x, y)
        new_left = new_left * scale
        new_right = new_right * scale
        m_ref[8 * s : 8 * s + 8, :128] = new_left
        m_ref[8 * s : 8 * s + 8, 128:] = new_right
        low = 8 * last
        if low < 128:
            update = t_dot(new_left, jnp.concatenate([new_left, new_right], axis=1))
            m_ref[low:, :] = m_ref[low:, :] - update[low:, :]


def identity(count, dtype=f32):
    row = lax.broadcasted_iota(jnp.int32, (count, count), 0)
    lane = lax.broadcasted_iota(jnp.int32, (count, count), 1)
    return jnp.where(row == lane, 1.0, 0.0).astype(dtype)


def eliminate(wide, small, r_ref, width):
    def step(p, carry):
        at = pl.multiple_of(p * 128, 128)
        small[:, :128] = wide[pl.ds(at, 128), pl.ds(at, 128)]
        small[:, 128:] = identity(128)
        factor_128(small)
        r_ref[:, :width] = dot(small[:, 128:], wide[pl.ds(at, 128), :width])
        wide[pl.ds(at, 128), :width] = r_ref[:, :width]

        def trail(q, carry):
            down = pl.multiple_of(q * 128, 128)
            wide[pl.ds(down, 128), :width] = wide[pl.ds(down, 128), :width] - t_dot(
                r_ref[:, pl.ds(down, 128)], r_ref[:, :width]
            )
            return carry

        lax.fori_loop(p + 1, 4, trail, 0)
        return carry

    lax.fori_loop(0, 4, step, 0)


def factor_pivots(x_in, x_out, fm, wide, small, r_ref):
    for p in range(8):
        wide[64 * p : 64 * p + 64, 0:512] = x_in[p, 0]
        wide[64 * p : 64 * p + 64, 512:1024] = x_in[p, 1]
    wide[:, 1024:] = identity(512)
    eliminate(wide, small, r_ref, 1536)
    for p in range(8):
        x_out[p, 0] = wide[64 * p : 64 * p + 64, 1024:]
        x_out[p, 1] = wide[64 * p : 64 * p + 64, 512:1024]
    u = wide[:, 512:1024]
    for i in range(2):
        product = t_dot(u[:, 256 * i : 256 * i + 256], u)
        for j in range(2):
            keep = fm[2 + i, 2 + j].astype(f32)
            for p in range(4):
                wide[256 * i + 64 * p : 256 * i + 64 * p + 64, 256 * j : 256 * j + 256] = (
                    x_in[4 * i + p, 2, :, 256 * j : 256 * j + 256]
                    - keep * product[64 * p : 64 * p + 64, 256 * j : 256 * j + 256]
                )
    wide[:, 512:1024] = identity(512)
    eliminate(wide, small, r_ref, 1024)
    for p in range(8):
        x_out[p, 2] = wide[64 * p : 64 * p + 64, 512:1024]


def exchange_kernel(
    tab, fm, child, front, kids, ar, ac, x3, panel,
    blocks, turned, e1s, e1r, e2s, bs, br, pf, pb, xs,
    e1_s, e1_r, e2_s, e2_r, b_s, b_r, c1_s, c1_r, c2_s, c2_r, c3_s, c3_r,
    d1_s, d1_r, d2_s, d2_r, x1_s, x1_r, x2_s, x2_r, x3_s, x3_r, here,
):
    r = lax.axis_index("row")
    c = lax.axis_index("col")
    h = c // 2
    core = lax.rem(c, 2)
    sibling = c + 1 - 2 * core

    def send(src, dst, ss, rs, row, col):
        return pltpu.make_async_remote_copy(
            src_ref=src, dst_ref=dst, send_sem=ss, recv_sem=rs,
            device_id=(row, col), device_id_type=MESH,
        )

    def each(low, high, body):
        def run(i, carry):
            body(i)
            return carry

        lax.fori_loop(low, high, run, 0)

    def greet(row, col):
        pl.semaphore_signal(
            pltpu.get_barrier_semaphore(), inc=1, device_id=(row, col), device_id_type=MESH
        )

    each(1, NR, lambda d: greet(lax.rem(r + d, NR), c))
    each(1, NC, lambda d: greet(r, lax.rem(c + d, NC)))

    @pl.when(c < 2)
    def _():
        each(1, NR, lambda d: greet(lax.rem(r + d, NR), 1 - c))

    @pl.when(c == 0)
    def _():
        pltpu.make_async_copy(front, pf, here.at[0]).start()

    pl.semaphore_wait(pltpu.get_barrier_semaphore(), jnp.where(c < 2, 29, 22))

    for a in range(16):
        blocks[a] = child[:, BS * a : BS * a + BS]

    @pl.when(c < 2)
    def _():
        one = identity(BS, bf16)

        def turn(a):
            turned[a] = dot_t(one, blocks[a], None).astype(bf16)

        each(0, 16, turn)

        def give(d):
            q = lax.rem(r + d, NR)
            for n in range(4):
                bs[q, n] = turned[tab[q] + n]

            @pl.when((q != r) | (c == 1))
            def _():
                send(bs.at[q], br.at[pl.ds(8 * r + 4 * c, 4)], b_s.at[q], b_r.at[2 * r + c], q, 0).start()

            @pl.when((q == r) & (c == 0))
            def _():
                for n in range(4):
                    br[8 * r + n] = bs[q, n]

        each(1, NR + 1, give)

    def to_col(d):
        q = lax.rem(c + d, NC)

        @pl.when((q >= 1) & (q <= h + 8))
        def _():
            @pl.when(q != c)
            def _():
                for n in range(2):
                    e1s[q, :, BS * n : BS * n + BS] = blocks[tab[8 + q] + n]
                send(e1s.at[q], e1r.at[c], e1_s.at[q], e1_r.at[c], r, q).start()

            @pl.when(q == c)
            def _():
                for n in range(2):
                    e1r[c, :, BS * n : BS * n + BS] = blocks[tab[8 + q] + n]

    each(1, NC + 1, to_col)

    @pl.when(c == 0)
    def _():
        pltpu.make_async_copy(front, pf, here.at[0]).wait()

        def arrive(k):
            @pl.when(k != 2 * r)
            def _():
                send(
                    bs.at[0], br.at[pl.ds(4 * k, 4)], b_s.at[0], b_r.at[k], k // 2, lax.rem(k, 2)
                ).wait_recv()

        each(0, 16, arrive)

        def assemble(i):
            def add(k):
                for j in range(4):
                    times = (tab[120 + 8 * k + i] * tab[184 + 4 * k + j]).astype(f32)
                    block = br[8 * k + 4 * tab[88 + 4 * k + j] + tab[24 + 8 * k + i]]
                    at = pl.ds(j * BS, BS)
                    pf[i, :, at] = pf[i, :, at] + times * block.astype(f32)

            each(0, NR, add)
            for j in range(4):
                at = pl.ds(j * BS, BS)
                kept = pf[i, :, at] * fm[8 * r + i, j].astype(f32)
                pf[i, :, at] = kept
                pb[i, 0, :, at] = kept[:128].astype(bf16)
                pb[i, 1, :, at] = kept[128:].astype(bf16)

        each(0, 8, assemble)
        pltpu.make_async_copy(pf, panel, here.at[0]).start()

        @pl.when(r == 0)
        def _():
            for p in range(8):
                i, low = p // 4, 64 * (p % 4)
                xs[p, 0] = pf[i, low : low + 64, 0:512]
                xs[p, 1] = pf[i, low : low + 64, 512:1024]
                xs[p, 2] = pf[i + 2, low : low + 64, 512:1024]

            each(1, NR, lambda q: send(xs.at[q], x3.at[q], x1_s.at[q], x1_r, q, 0).start())
            each(1, NC, lambda q: send(xs.at[0], x3.at[0], x2_s.at[q], x2_r, 0, q).start())
            each(1, NR, lambda q: send(xs.at[0], x3.at[0], x3_s.at[q], x3_r.at[0], q, 0).start())
            pltpu.make_async_copy(xs, x3, here.at[1]).start()

        each(
            1, NC,
            lambda q: send(
                pb.at[q // 2, lax.rem(q, 2)], ar.at[q // 2, lax.rem(q, 2)], c1_s.at[q], c1_r, r, q
            ).start(),
        )
        each(
            1, 8,
            lambda q: send(pb.at[0, 0], ar.at[0, 0], c2_s.at[q], c2_r.at[0], r, 2 * q).start(),
        )
        each(
            0, 8,
            lambda q: send(pb.at[q, 0], ar.at[q, 0], c3_s.at[q], c3_r.at[q], r, 1).start(),
        )

        @pl.when(r > 0)
        def _():
            send(x3.at[r], x3.at[r], x1_s.at[0], x1_r, 0, 0).wait_recv()
            each(1, NC, lambda q: send(x3.at[r], x3.at[r], x2_s.at[q], x2_r, r, q).start())

            def on(q):
                @pl.when(q != r)
                def _():
                    send(x3.at[r], x3.at[r], x3_s.at[q], x3_r.at[r], q, 0).start()

            each(1, NR, on)

    @pl.when(c > 0)
    def _():
        def arrive(a):
            @pl.when(a != c)
            def _():
                send(e1s.at[0], e1r.at[a], e1_s.at[0], e1_r.at[a], r, a).wait_recv()

        each(jnp.maximum(2 * (c - 8), 0), NC, arrive)

        def to_row(d):
            q = lax.rem(r + d, NR)

            @pl.when(q >= h)
            def _():
                for n in range(4):
                    e2s[q, n] = e1r[tab[q] + n]

                @pl.when(q != r)
                def _():
                    send(e2s.at[q], kids.at[r], e2_s.at[q], e2_r.at[r], q, c).start()

                @pl.when(q == r)
                def _():
                    pltpu.make_async_copy(e2s.at[q], kids.at[r], here.at[2]).start()

        each(1, NR + 1, to_row)

        send(ar.at[h, core], ar.at[h, core], c1_s.at[0], c1_r, r, 0).wait_recv()

        def spread(d):
            q = lax.rem(h + d, 8)

            @pl.when((q != 0) | (core != 0))
            def _():
                send(
                    ar.at[h, core], ar.at[h, core], c2_s.at[q], c2_r.at[h], r, 2 * q + core
                ).start()

        each(1, 8, spread)

        def across(q):
            @pl.when(c != 1)
            def _():
                send(ar.at[q, core], ar.at[q, core], c3_s.at[q], c3_r.at[q], r, sibling).start()

        across(h)

        send(x3.at[r], x3.at[r], x2_s.at[0], x2_r, r, 0).wait_recv()
        each(
            1, NR,
            lambda d: send(
                x3.at[r], x3.at[r], x3_s.at[lax.rem(r + d, NR)], x3_r.at[r], lax.rem(r + d, NR), c
            ).start(),
        )

        def collect(d):
            q = lax.rem(h + d, 8)
            send(
                ar.at[q, core], ar.at[q, core], c2_s.at[q], c2_r.at[q], r, 2 * q + core
            ).wait_recv()
            across(q)

        each(1, 8, collect)
        each(
            0, 8,
            lambda q: send(
                ar.at[q, 1 - core], ar.at[q, 1 - core], c3_s.at[q], c3_r.at[q], r, sibling
            ).wait_recv(),
        )

        @pl.when(r == h)
        def _():
            pltpu.make_async_copy(ar.at[pl.ds(4 * core, 4)], ac, here.at[3]).start()

            def scatter(d):
                q = lax.rem(r + d, NR)
                send(
                    ar.at[4 * core + q // 2, lax.rem(q, 2)], ac.at[q // 2, lax.rem(q, 2)],
                    d1_s.at[q], d1_r, q, c,
                ).start()

            each(1, NR, scatter)
            each(
                r + 1, NR,
                lambda q: send(
                    ar.at[4 * core + r // 2, lax.rem(r, 2)], ac.at[r // 2, lax.rem(r, 2)],
                    d2_s.at[q], d2_r.at[r], q, c,
                ).start(),
            )

        @pl.when(r != h)
        def _():
            mine = ac.at[r // 2, lax.rem(r, 2)]
            send(mine, mine, d1_s.at[0], d1_r, h, c).wait_recv()

            def on(q):
                @pl.when(q != r)
                def _():
                    send(mine, mine, d2_s.at[q], d2_r.at[r], q, c).start()

            each(h + 1, NR, on)

        @pl.when(r > h)
        def _():
            def arrive(q):
                @pl.when(q != r)
                def _():
                    at = ac.at[q // 2, lax.rem(q, 2)]
                    send(at, at, d2_s.at[q], d2_r.at[q], q, c).wait_recv()

            each(0, NR, arrive)

        @pl.when(r >= h)
        def _():
            def arrive(q):
                @pl.when(q != r)
                def _():
                    send(e2s.at[0], kids.at[q], e2_s.at[0], e2_r.at[q], q, c).wait_recv()

            each(0, NR, arrive)

    @pl.when((c > 0) | (r > 0))
    def _():
        def arrive(q):
            @pl.when(q != r)
            def _():
                send(x3.at[q], x3.at[q], x3_s.at[q], x3_r.at[q], q, c).wait_recv()

        each(0, NR, arrive)

    def sent(buffer, sem):
        send(buffer, buffer, sem, c1_r, r, sibling).wait_send()

    @pl.when(c < 2)
    def _():
        def left(q):
            @pl.when((q != r) | (c == 1))
            def _():
                sent(bs.at[q], b_s.at[q])

        each(0, NR, left)

    def left_col(q):
        @pl.when((q >= 1) & (q <= h + 8) & (q != c))
        def _():
            sent(e1s.at[q], e1_s.at[q])

    each(0, NC, left_col)

    @pl.when(c == 0)
    def _():
        pltpu.make_async_copy(pf, panel, here.at[0]).wait()

        @pl.when(r == 0)
        def _():
            pltpu.make_async_copy(xs, x3, here.at[1]).wait()
            each(1, NR, lambda q: sent(xs.at[q], x1_s.at[q]))

        each(1, NC, lambda q: sent(pb.at[0, 0], c1_s.at[q]))
        each(1, 8, lambda q: sent(pb.at[0, 0], c2_s.at[q]))
        each(0, 8, lambda q: sent(pb.at[q, 0], c3_s.at[q]))
        each(1, NC, lambda q: sent(xs.at[0], x2_s.at[q]))

        def left(q):
            @pl.when(q != r)
            def _():
                sent(xs.at[0], x3_s.at[q])

        each(1, NR, left)

    @pl.when(c > 0)
    def _():
        def left_row(q):
            @pl.when(q != r)
            def _():
                sent(e2s.at[q], e2_s.at[q])

            @pl.when(q == r)
            def _():
                pltpu.make_async_copy(e2s.at[q], kids.at[r], here.at[2]).wait()

        each(h, NR, left_row)

        def left_spread(q):
            @pl.when((q != h) & ((q != 0) | (core != 0)))
            def _():
                sent(ar.at[0, 0], c2_s.at[q])

        each(0, 8, left_spread)

        @pl.when(c != 1)
        def _():
            each(0, 8, lambda q: sent(ar.at[0, 0], c3_s.at[q]))

        each(1, NR, lambda d: sent(x3.at[0], x3_s.at[lax.rem(r + d, NR)]))

        @pl.when(r == h)
        def _():
            pltpu.make_async_copy(ar.at[pl.ds(4 * core, 4)], ac, here.at[3]).wait()
            each(1, NR, lambda d: sent(ar.at[0, 0], d1_s.at[lax.rem(r + d, NR)]))
            each(r + 1, NR, lambda q: sent(ar.at[0, 0], d2_s.at[q]))

        @pl.when(r != h)
        def _():
            def left(q):
                @pl.when(q != r)
                def _():
                    sent(ac.at[0, 0], d2_s.at[q])

            each(h + 1, NR, left)


def exchange(tab, fm, child, front):
    dma = pltpu.SemaphoreType.DMA
    sds = jax.ShapeDtypeStruct
    return pl.pallas_call(
        exchange_kernel,
        in_specs=[SM, SM, VM, ANY],
        out_specs=[ANY] * 5,
        out_shape=[
            sds((NR, 4, BS, 2 * BS), bf16),
            sds((8, 2, 128, 1024), bf16),
            sds((4, 2, 128, 1024), bf16),
            sds((8, 3, 64, 512), f32),
            sds((8, BS, 1024), f32),
        ],
        scratch_shapes=[
            pltpu.VMEM((16, BS, BS), bf16),
            pltpu.VMEM((16, BS, BS), bf16),
            pltpu.VMEM((NC, BS, 2 * BS), bf16),
            pltpu.VMEM((NC, BS, 2 * BS), bf16),
            pltpu.VMEM((NR, 4, BS, 2 * BS), bf16),
            pltpu.VMEM((NR, 4, BS, BS), bf16),
            pltpu.VMEM((64, BS, BS), bf16),
            pltpu.VMEM((8, BS, 1024), f32),
            pltpu.VMEM((8, 2, 128, 1024), bf16),
            pltpu.VMEM((8, 3, 64, 512), f32),
            dma((NC,)), dma((NC,)), dma((NR,)), dma((NR,)), dma((NR,)), dma((16,)),
            dma((NC,)), dma, dma((8,)), dma((8,)), dma((8,)), dma((8,)),
            dma((NR,)), dma, dma((NR,)), dma((NR,)),
            dma((NR,)), dma, dma((NC,)), dma, dma((NR,)), dma((NR,)), dma((4,)),
        ],
        compiler_params=pltpu.CompilerParams(
            collective_id=1, has_side_effects=True, vmem_limit_bytes=56 << 20
        ),
        cost_estimate=pl.CostEstimate(flops=0, bytes_accessed=400_000_000, transcendentals=0),
        name="exchange",
    )(tab, fm, child, front)


def pivots(fm, x3):
    return pl.pallas_call(
        factor_pivots_kernel,
        in_specs=[SM, VM],
        out_specs=VM,
        out_shape=jax.ShapeDtypeStruct((8, 3, 64, 512), f32),
        scratch_shapes=[
            pltpu.VMEM((512, 1536), f32),
            pltpu.VMEM((128, 256), f32),
            pltpu.VMEM((128, 1536), f32),
        ],
        compiler_params=pltpu.CompilerParams(vmem_limit_bytes=32 << 20),
        name="pivots",
    )(fm, x3)


def factor_pivots_kernel(fm, x_in, x_out, wide, small, r_ref):
    factor_pivots(x_in, x_out, fm, wide, small, r_ref)


def update_kernel(
    tab, fm, front, panel, ar, ac, x3, kids, out, inv0, low, inv1, wc,
):
    r = lax.axis_index("row")
    c = lax.axis_index("col")
    i = pl.program_id(0)
    g = 8 * r + i
    active = g >= 4 * c

    def gather(n, dtype):
        return jnp.concatenate([x3[p, n] for p in range(8)], axis=0).astype(dtype)

    def solve(rows0, rows1, block_row):
        first = dot_t(rows0, inv0[...], None).astype(bf16)
        across = dot(first, low[...], None)
        second = jnp.concatenate(
            [
                rows1[:, BS * j : BS * j + BS].astype(f32)
                - fm[block_row, 2 + j].astype(f32) * across[:, BS * j : BS * j + BS]
                for j in range(2)
            ],
            axis=1,
        ).astype(bf16)
        return first, dot_t(second, inv1[...], None).astype(bf16)

    @pl.when((i == 0) & (c > 0) & (h_of(c) <= r))
    def _():
        inv0[...] = gather(0, bf16)
        low[...] = gather(1, bf16)
        inv1[...] = gather(2, bf16)
        for j in range(4):
            block = jnp.concatenate([ac[j, 0], ac[j, 1]], axis=0)
            first, second = solve(block[:, :512], block[:, 512:], 4 * c + j)
            wc[BS * j : BS * j + BS, :512] = first
            wc[BS * j : BS * j + BS, 512:] = second

    @pl.when(jnp.logical_not(active))
    def _():
        out[...] = jnp.zeros_like(out)

    @pl.when(active & (c == 0))
    def _():
        first = dot_t(panel[0, :, :512], gather(0, f32))
        across = dot(first, gather(1, f32))
        second = jnp.concatenate(
            [
                panel[0, :, 512 + BS * j : 768 + BS * j]
                - fm[g, 2 + j].astype(f32) * across[:, BS * j : BS * j + BS]
                for j in range(2)
            ],
            axis=1,
        )
        second = dot_t(second, gather(2, f32))
        row = g * BS + lax.broadcasted_iota(jnp.int32, (BS, 512), 0)
        lane = lax.broadcasted_iota(jnp.int32, (BS, 512), 1)
        out[:, :512] = jnp.where(row >= lane, first, 0.0)
        out[:, 512:] = jnp.where(row >= lane + 512, second, 0.0)

    @pl.when(active & (c > 0))
    def _():
        block = jnp.concatenate([ar[0, 0], ar[0, 1]], axis=0)
        first, second = solve(block[:, :512], block[:, 512:], g)
        for j in range(4):
            at = pl.ds(BS * j, BS)
            keep = (fm[g, 4 * c + j] != 0) & (g >= 4 * c + j)

            @pl.when(keep)
            def _():
                product = dot_t(first, wc[BS * j : BS * j + BS, :512], None) + dot_t(
                    second, wc[BS * j : BS * j + BS, 512:], None
                )
                times = fm[g, 4 * c + j].astype(f32)
                out[:, at] = (front[:, at] - product) * times

                for k in range(NR):
                    slot = tab[24 + 8 * k + i]
                    side = tab[88 + 4 * k + j]

                    @pl.when(tab[120 + 8 * k + i] * tab[184 + 4 * k + j] > 0)
                    def _():
                        from_col = pl.multiple_of(side * BS, BS)
                        out[:, at] = out[:, at] + times * kids[
                            k, slot, :, pl.ds(from_col, BS)
                        ].astype(f32)

            @pl.when(jnp.logical_not(keep))
            def _():
                out[:, at] = jnp.zeros((BS, BS), f32)


def h_of(c):
    return c // 2


def update(tab, fm, front, panel, ar, ac, x3, kids):
    whole = lambda shape: pl.BlockSpec(
        shape, lambda i: (0,) * len(shape), pipeline_mode=pl.Buffered(1)
    )
    return pl.pallas_call(
        update_kernel,
        grid=(8,),
        in_specs=[
            SM, SM,
            pl.BlockSpec((BS, 1024), lambda i: (i, 0)),
            pl.BlockSpec((1, BS, 1024), lambda i: (i, 0, 0)),
            pl.BlockSpec((1, 2, 128, 1024), lambda i: (i, 0, 0, 0)),
            whole((4, 2, 128, 1024)),
            whole((8, 3, 64, 512)),
            whole((NR, 4, BS, 2 * BS)),
        ],
        out_specs=pl.BlockSpec((BS, 1024), lambda i: (i, 0)),
        out_shape=jax.ShapeDtypeStruct((2048, 1024), f32),
        scratch_shapes=[
            pltpu.VMEM((512, 512), bf16),
            pltpu.VMEM((512, 512), bf16),
            pltpu.VMEM((512, 512), bf16),
            pltpu.VMEM((1024, 1024), bf16),
        ],
        compiler_params=pltpu.CompilerParams(vmem_limit_bytes=48 << 20),
        name="update",
    )(tab, fm, front, panel, ar, ac, x3, kids)


def tables(maps, r, c):
    own = lax.dynamic_index_in_dim(maps, r, 0, keepdims=False)
    row_start = jnp.minimum(jnp.sum(own[:, None] < 8 * jnp.arange(NR), axis=0), 12)
    col_start = jnp.minimum(jnp.sum(own[:, None] < 4 * jnp.arange(NC), axis=0), 14)
    index = jnp.arange(16)
    rows = maps[:, None, :] == 8 * r + jnp.arange(8)[None, :, None]
    row_first = jnp.minimum(jnp.sum(maps < 8 * r, axis=1), 12)
    row_slot = jnp.sum(rows * (index - row_first[:, None, None] + 1), axis=-1) - 1
    cols = maps[:, None, :] == 4 * c + jnp.arange(4)[None, :, None]
    col_first = jnp.minimum(jnp.sum(maps < 4 * c, axis=1), 14)
    col_slot = jnp.sum(cols * (index - col_first[:, None, None] + 1), axis=-1) - 1
    parts = [
        row_start,
        col_start,
        jnp.maximum(row_slot, 0).reshape(-1),
        jnp.maximum(col_slot, 0).reshape(-1),
        (row_slot >= 0).reshape(-1),
        (col_slot >= 0).reshape(-1),
    ]
    parts = [part.astype(jnp.int32) for part in parts]
    return jnp.concatenate(parts)


def local(front, child_updates, child_maps, fill_mask):
    r = lax.axis_index("row")
    c = lax.axis_index("col")
    tab = tables(child_maps, r, c)
    kids, ar, ac, x3, panel = exchange(
        tab, fill_mask, child_updates[0], front.reshape(8, BS, 1024)
    )
    x3 = pivots(fill_mask, x3)
    return update(tab, fill_mask, front, panel, ar, ac, x3, kids)


def solution(mesh):
    placed = (P("row", "col"), P("row", "col", None), P(), P())
    return jax.shard_map(
        local, mesh=mesh, in_specs=placed, out_specs=P("row", "col"), check_vma=False
    )
```

time: 1300 us -> 391 us (0.30)
  the two profiles are of different devices: /device:TPU:112 before, /device:TPU:1 now
where the time goes in v1:
time: 391 us
  Pallas kernels  384 us (98%)
    pallas_call x1, Pallas kernels, exchange(): pl.pallas_call(exchange_kernel, in_specs=[SM, SM, VM, ANY], out_specs=[AN...  311 us
    pallas_call x1, Pallas kernels, pivots(): pl.pallas_call(factor_pivots_kernel, in_specs=[SM, VM], out_specs=VM, out...  52 us
    pallas_call x1, Pallas kernels, update(): pl.pallas_call(update_kernel, grid=(8,), in_specs=[SM, SM, pl.BlockSpec((...  20.4 us

profile of v1, /device:TPU:1, one launch (start us, length us, event | category | flops | bytes accessed | tf_op | source)
XLA Modules:
  0.0 390.9 jit_solution(6027240116165966048)
XLA Ops:
  0.0 0.7 dynamic-slice_bitcast_fusion
  0.7 0.8 convert_reduce_fusion.1
  1.6 0.2 convert_reduce_fusion.3
  1.8 0.1 convert_reduce_fusion
  1.8 0.1 subtract_add_fusion
  1.9 0.9 select_reduce_fusion.1
  2.8 0.1 copy.5
  2.9 0.1 max.17
  3.0 0.1 copy.6
  3.1 0.1 reshape.104
  3.2 0.1 subtract_add_fusion.1
  3.2 1.0 select_reduce_fusion
  4.2 0.1 reshape.103
  4.3 0.1 max.15
  4.4 0.7 concatenate.3.tab
  5.1 0.0 copy-start.2
  5.1 311.4 %exchange.1 = (bf16[8,4,256,512]{3,2,1,0:T(8,128)(2,1)}, bf16[8,2,128,1024]{3,2,1,0:T(8,128)(2,1)}, bf16[4,2,128,1024]{3,2,1,0:T(8,128)(2,1)}, f32[8,3,64,512]{3,2,1,0:T(8,128)}, f32[8,256,1024]{2,1,0:T(8,128)}) custom-call(s32[216]{0:T(256)} %concatenate.3.tab, s32[64,64]{1,0:T(8,128)} %fm.5, bf16[256,4096]{1,0:T(8,128)(2,1)} %bitcast.5, ...), custom_call_target="tpu_custom_call" | custom-call | bytes 400000000 | tf_op jit(solution)/shard_map/exchange/pallas_call | solution.py:533
  316.5 0.0 copy-start.3
  316.5 0.0 copy-done.2
  316.5 0.0 copy-start
  316.5 1.9 copy-done
  318.4 0.0 copy-start.1
  318.4 52.0 %pivots.1.x3 = f32[8,3,64,512]{3,2,1,0:T(8,128)S(1)} custom-call(s32[64,64]{1,0:T(8,128)S(1)} %copy-done.2, f32[8,3,64,512]{3,2,1,0:T(8,128)S(1)} %copy-done), custom_call_target="tpu_custom_call" | custom-call | tf_op jit(solution)/shard_map/pivots/pallas_call | solution.py:569
  370.4 0.0 copy-done.3
  370.4 0.0 copy-done.1
  370.4 20.4 %update.1 = f32[2048,1024]{1,0:T(8,128)} custom-call(s32[216]{0:T(256)S(1)} %copy-done.3, s32[64,64]{1,0:T(8,128)S(1)} %copy-done.2, f32[2048,1024]{1,0:T(8,128)} %front.1, f32[8,256,1024]{2,1,0:T(8,128)} %get-tuple-element.10.panel, bf16[8,2,128,1024]{3,2,1,0:T(8,128)(2,1)} %get-tuple-element.11.ar, bf16[4,2,128,1024]{3,2,1,0:T(8,128)(2,1)S(1)} %copy-done.1, ...), custom_call_target="tpu_custom_call" | custom-call | tf_op jit(solution)/shard_map/update/pallas_call | solution.py:686
  (11 shorter events, 0.1 us)
Async XLA Ops:
  5.1 311.5 %copy-start.2 = (s32[64,64]{1,0:T(8,128)S(1)}, s32[64,64]{1,0:T(8,128)}, u32[]{:S(2)}) copy-start(s32[64,64]{1,0:T(8,128)} %fm.5) | copy-start | bytes 49156
  316.5 53.9 %copy-start.3 = (s32[216]{0:T(256)S(1)}, s32[216]{0:T(256)}, u32[]{:S(2)}) copy-start(s32[216]{0:T(256)} %concatenate.3.tab) | copy-start | bytes 2596
  316.5 1.9 copy-start
  318.4 52.0 %copy-start.1 = (bf16[4,2,128,1024]{3,2,1,0:T(8,128)(2,1)S(1)}, bf16[4,2,128,1024]{3,2,1,0:T(8,128)(2,1)}, u32[]{:S(2)}) copy-start(bf16[4,2,128,1024]{3,2,1,0:T(8,128)(2,1)} %get-tuple-element.12.ac) | copy-start | bytes 6291460

commit v2 on v1

v2 whole, which is shorter than its diff:
```python
import functools

import jax
import jax.numpy as jnp
from jax import lax
from jax.experimental import pallas as pl
from jax.experimental.pallas import tpu as pltpu
from jax.sharding import PartitionSpec as P

BS = 256
NR = 8
NC = 16
MESH = pl.DeviceIdType.MESH
HI = lax.Precision.HIGHEST
f32 = jnp.float32
bf16 = jnp.bfloat16
ANY = pl.BlockSpec(memory_space=pl.ANY)
VM = pl.BlockSpec(memory_space=pltpu.VMEM)
SM = pl.BlockSpec(memory_space=pltpu.SMEM)


def dot(a, b, precision=HI):
    return lax.dot_general(
        a, b, (((1,), (0,)), ((), ())), precision=precision, preferred_element_type=f32
    )


def dot_t(a, b, precision=HI):
    return lax.dot_general(
        a, b, (((1,), (1,)), ((), ())), precision=precision, preferred_element_type=f32
    )


def t_dot(a, b, precision=HI):
    return lax.dot_general(
        a, b, (((0,), (0,)), ((), ())), precision=precision, preferred_element_type=f32
    )


def row_of(x, k):
    return jnp.broadcast_to(x[k : k + 1, :], (8, 128))


def lane_of(x, k):
    return jnp.broadcast_to(x[:, k : k + 1], (8, 128))


def factor_128(m_ref, ahead=3):
    sub = lax.broadcasted_iota(jnp.int32, (8, 128), 0)
    lane = lax.broadcasted_iota(jnp.int32, (8, 128), 1)
    held = {}
    for s in range(16):
        last = min(s + ahead + 1, 16)
        for q in range(s, last):
            if q not in held:
                held[q] = (m_ref[8 * q : 8 * q + 8, :128], m_ref[8 * q : 8 * q + 8, 128:])
        left, right = held.pop(s)
        v = [lane_of(left, 8 * s + j) for j in range(8)]
        z = [jnp.where(sub == j, 1.0, 0.0).astype(f32) for j in range(8)]
        scale = jnp.zeros((8, 128), f32)
        rows, inverses = [], []
        for k in range(8):
            root = lax.rsqrt(row_of(v[k], k))
            scale = jnp.where(sub == k, root, scale)
            inverse = root * root
            inverses.append(inverse)
            below = jnp.where(sub > k, v[k], 0.0) * inverse
            row = {}
            for j in range(k + 1, 8):
                row[j] = row_of(v[j], k)
                v[j] = v[j] - below * row[j]
            rows.append(row)
            if k < 7:
                for j in range(k + 1):
                    z[j] = z[j] - below * row_of(z[j], k)
        new_left = z[0] * row_of(left, 0)
        new_right = z[0] * row_of(right, 0)
        for j in range(1, 8):
            new_left = new_left + z[j] * row_of(left, j)
            new_right = new_right + z[j] * row_of(right, j)
        new_left = jnp.where(lane >= 8 * s + sub, new_left, 0.0)
        rows_left = [row_of(new_left, k) for k in range(8)]
        rows_right = [row_of(new_right, k) for k in range(8)]
        for q in range(s + 1, last):
            x, y = held[q]
            w = [lane_of(x, 8 * s + j) for j in range(8)]
            for k in range(8):
                times = w[k] * inverses[k]
                for j in range(k + 1, 8):
                    w[j] = w[j] - times * rows[k][j]
                x = x - times * rows_left[k]
                y = y - times * rows_right[k]
            held[q] = (x, y)
        new_left = new_left * scale
        new_right = new_right * scale
        m_ref[8 * s : 8 * s + 8, :128] = new_left
        m_ref[8 * s : 8 * s + 8, 128:] = new_right
        low = 8 * last
        if low < 128:
            update = t_dot(new_left, jnp.concatenate([new_left, new_right], axis=1))
            m_ref[low:, :] = m_ref[low:, :] - update[low:, :]


def identity(count, dtype=f32):
    row = lax.broadcasted_iota(jnp.int32, (count, count), 0)
    lane = lax.broadcasted_iota(jnp.int32, (count, count), 1)
    return jnp.where(row == lane, 1.0, 0.0).astype(dtype)


def eliminate(wide, small, r_ref, width):
    def step(p, carry):
        at = pl.multiple_of(p * 128, 128)
        small[:, :128] = wide[pl.ds(at, 128), pl.ds(at, 128)]
        small[:, 128:] = identity(128)
        factor_128(small)
        r_ref[:, :width] = dot(small[:, 128:], wide[pl.ds(at, 128), :width])
        wide[pl.ds(at, 128), :width] = r_ref[:, :width]

        def trail(q, carry):
            down = pl.multiple_of(q * 128, 128)
            wide[pl.ds(down, 128), :width] = wide[pl.ds(down, 128), :width] - t_dot(
                r_ref[:, pl.ds(down, 128)], r_ref[:, :width]
            )
            return carry

        lax.fori_loop(p + 1, 4, trail, 0)
        return carry

    lax.fori_loop(0, 4, step, 0)


def first_pivot(x3, wide, small, r_ref):
    for p in range(8):
        wide[64 * p : 64 * p + 64, 0:512] = x3[p, 0]
        wide[64 * p : 64 * p + 64, 512:1024] = x3[p, 1]
    wide[:, 1024:] = identity(512)
    eliminate(wide, small, r_ref, 1536)
    for p in range(8):
        x3[p, 0] = wide[64 * p : 64 * p + 64, 1024:]
        x3[p, 1] = wide[64 * p : 64 * p + 64, 512:1024]


def second_matrix(x3, fm, wide):
    u = wide[:, 512:1024]
    for i in range(2):
        product = t_dot(u[:, 256 * i : 256 * i + 256], u)
        for j in range(2):
            keep = fm[2 + i, 2 + j].astype(f32)
            for p in range(4):
                wide[256 * i + 64 * p : 256 * i + 64 * p + 64, 256 * j : 256 * j + 256] = (
                    x3[4 * i + p, 2, :, 256 * j : 256 * j + 256]
                    - keep * product[64 * p : 64 * p + 64, 256 * j : 256 * j + 256]
                )
    wide[:, 512:1024] = identity(512)


def second_pivot(x3, wide, small, r_ref):
    eliminate(wide, small, r_ref, 1024)
    for p in range(8):
        x3[p, 2] = wide[64 * p : 64 * p + 64, 512:1024]


def exchange_kernel(
    tab, fm, child, front, kids, ar_out, ac_out, xb_out, x3_out, panel,
    blocks, turned, e1s, e1r, wide_kids, bs, pf, ar, ac, x3, xb, wide, small, r_ref,
    k_s, k_r, e1_s, e1_r, e2_s, e2_r, b_s, b_r, c1_s, c1_r, c2_s, c2_r, c3_s, c3_r,
    d1_s, d1_r, d2_s, d2_r, x1_s, x1_r, x2_s, x2_r, x3_s, x3_r, here,
):
    r = lax.axis_index("row")
    c = lax.axis_index("col")
    h = c // 2
    core = lax.rem(c, 2)
    sibling = c + 1 - 2 * core
    root = (r == 0) & (c == 0)
    barrier = pltpu.get_barrier_semaphore()

    def send(src, dst, ss, rs, row, col):
        return pltpu.make_async_remote_copy(
            src_ref=src, dst_ref=dst, send_sem=ss, recv_sem=rs,
            device_id=(row, col), device_id_type=MESH,
        )

    def move(src, dst, n):
        return pltpu.make_async_copy(src, dst, here.at[n])

    def each(low, high, body):
        def run(i, carry):
            body(i)
            return carry

        lax.fori_loop(low, high, run, 0)

    def when(condition, body):
        pl.when(condition)(body)

    def greet(row, col):
        pl.semaphore_signal(barrier, inc=1, device_id=(row, col), device_id_type=MESH)

    each(1, NR, lambda d: greet(lax.rem(r + d, NR), c))
    each(1, NC, lambda d: greet(r, lax.rem(c + d, NC)))

    @pl.when(c < 2)
    def _():
        each(1, NR, lambda d: greet(lax.rem(r + d, NR), 1 - c))

    @pl.when(c == 0)
    def _():
        move(front.at[pl.ds(0, 4)], pf.at[pl.ds(0, 4)], 0).start()
        move(front.at[pl.ds(4, 4)], pf.at[pl.ds(4, 4)], 3).start()

    for a in range(16):
        blocks[a] = child[:, BS * a : BS * a + BS]

    def turn(a):
        turned[a] = dot_t(identity(BS, bf16), blocks[a], None).astype(bf16)

    when(c < 2, lambda: each(0, 16, turn))
    pl.semaphore_wait(barrier, jnp.where(c < 2, 29, 22))

    @pl.when((c < 2) & jnp.logical_not(root))
    def _():
        send(turned.at[pl.ds(0, 2)], e1r.at[2 * r + c], k_s, k_r.at[2 * r + c], 0, 0).start()

    @pl.when(root)
    def _():
        for n in range(2):
            e1r[0, n] = turned[n]

    @pl.when(c < 2)
    def _():
        def give(d):
            q = lax.rem(r + d, NR)
            for n in range(4):
                bs[q, n] = turned[tab[q] + n]

            @pl.when((q != r) | (c == 1))
            def _():
                send(
                    bs.at[q], wide_kids.at[pl.ds(8 * r + 4 * c, 4)],
                    b_s.at[q], b_r.at[2 * r + c], q, 0,
                ).start()

            @pl.when((q == r) & (c == 0))
            def _():
                for n in range(4):
                    wide_kids[8 * r + n] = bs[q, n]

        each(1, NR + 1, give)

    def to_col(d):
        q = lax.rem(c + d, NC)

        @pl.when((q >= 1) & (q <= h + 8))
        def _():
            @pl.when(q != c)
            def _():
                for n in range(2):
                    e1s[q, n] = blocks[tab[8 + q] + n]
                send(e1s.at[q], e1r.at[c], e1_s.at[q], e1_r.at[c], r, q).start()

            @pl.when(q == c)
            def _():
                for n in range(2):
                    e1r[c, n] = blocks[tab[8 + q] + n]

    each(1, NC + 1, to_col)

    def assemble_panel():
        move(front.at[pl.ds(0, 4)], pf.at[pl.ds(0, 4)], 3).wait()

        def arrive(k):
            @pl.when(k != 2 * r)
            def _():
                send(
                    bs.at[0], wide_kids.at[pl.ds(4 * k, 4)],
                    b_s.at[0], b_r.at[k], k // 2, lax.rem(k, 2),
                ).wait_recv()

        each(0, 16, arrive)

        def assemble(i):
            def add(k):
                for j in range(4):
                    times = (tab[120 + 8 * k + i] * tab[184 + 4 * k + j]).astype(f32)
                    block = wide_kids[8 * k + 4 * tab[88 + 4 * k + j] + tab[24 + 8 * k + i]]
                    at = pl.ds(j * BS, BS)
                    pf[i, :, at] = pf[i, :, at] + times * block.astype(f32)

            each(0, NR, add)
            for j in range(4):
                at = pl.ds(j * BS, BS)
                kept = pf[i, :, at] * fm[8 * r + i, j].astype(f32)
                pf[i, :, at] = kept
                ar[i, 0, :, at] = kept[:128].astype(bf16)
                ar[i, 1, :, at] = kept[128:].astype(bf16)

        each(0, 8, assemble)
        move(pf, panel, 0).start()

    @pl.when(root)
    def _():
        move(front.at[pl.ds(0, 4)], pf.at[pl.ds(0, 4)], 0).wait()
        each(1, 16, lambda k: send(
            turned.at[pl.ds(0, 2)], e1r.at[k], k_s, k_r.at[k], k // 2, lax.rem(k, 2)
        ).wait_recv())
        for n, rows, cols in ((0, 0, 0), (1, 0, 2), (2, 2, 2)):
            for i in range(2):
                for j in range(2):
                    for p in range(4):
                        x3[4 * i + p, n, :, BS * j : BS * j + BS] = pf[
                            rows + i, 64 * p : 64 * p + 64,
                            BS * (cols + j) : BS * (cols + j) + BS,
                        ]

                    def add(k):
                        times = (
                            tab[120 + 8 * k + rows + i] * tab[184 + 4 * k + cols + j]
                        ).astype(f32)
                        block = e1r[
                            2 * k + tab[88 + 4 * k + cols + j], tab[24 + 8 * k + rows + i]
                        ].astype(f32) * times
                        for p in range(4):
                            at = pl.ds(BS * j, BS)
                            x3[4 * i + p, n, :, at] = (
                                x3[4 * i + p, n, :, at] + block[64 * p : 64 * p + 64]
                            )

                    each(0, NR, add)
                    keep = fm[rows + i, cols + j].astype(f32)
                    for p in range(4):
                        at = pl.ds(BS * j, BS)
                        x3[4 * i + p, n, :, at] = x3[4 * i + p, n, :, at] * keep
        first_pivot(x3, wide, small, r_ref)
        second_matrix(x3, fm, wide)
        assemble_panel()
        send(ar, ar, c1_s.at[1], c1_r, 0, 1).start()
        second_pivot(x3, wide, small, r_ref)
        each(1, NR, lambda q: send(x3.at[q], x3.at[q], x1_s.at[q], x1_r, q, 0).start())

    @pl.when((c == 0) & (r > 0))
    def _():
        move(front.at[pl.ds(0, 4)], pf.at[pl.ds(0, 4)], 0).wait()
        assemble_panel()
        each(1, NC, lambda q: send(
            ar.at[q // 2, lax.rem(q, 2)], ar.at[q // 2, lax.rem(q, 2)], c1_s.at[q], c1_r, r, q
        ).start())
        each(1, 8, lambda q: send(
            ar.at[0, 0], ar.at[0, 0], c2_s.at[q], c2_r.at[0], r, 2 * q
        ).start())
        each(0, 8, lambda q: send(
            ar.at[q, 0], ar.at[q, 0], c3_s.at[q], c3_r.at[q], r, 1
        ).start())
        send(x3.at[r], x3.at[r], x1_s.at[0], x1_r, 0, 0).wait_recv()

    @pl.when(c == 0)
    def _():
        xb[r] = x3[r].astype(bf16)
        each(1, NC, lambda q: send(xb.at[r], xb.at[r], x2_s.at[q], x2_r, r, q).start())

        def on(q):
            @pl.when(q != r)
            def _():
                send(x3.at[r], x3.at[r], x3_s.at[q], x3_r.at[r], q, 0).start()

        each(1, NR, on)

    @pl.when(c > 0)
    def _():
        def arrive(a):
            @pl.when(a != c)
            def _():
                send(e1s.at[0], e1r.at[a], e1_s.at[0], e1_r.at[a], r, a).wait_recv()

        each(jnp.maximum(2 * (c - 8), 0), NC, arrive)

        def to_row(d):
            q = lax.rem(r + ORDER(d), NR)

            @pl.when(q >= h)
            def _():
                for n in range(4):
                    for m in range(2):
                        wide_kids[8 * q + 4 * m + n] = e1r[tab[q] + n, m]

                @pl.when(q != r)
                def _():
                    send(
                        wide_kids.at[pl.ds(8 * q, 8)], kids.at[r], e2_s.at[q], e2_r.at[r], q, c
                    ).start()

                @pl.when(q == r)
                def _():
                    move(wide_kids.at[pl.ds(8 * q, 8)], kids.at[r], 2).start()

        each(1, NR + 1, to_row)

    @pl.when((r == 0) & (c == 1))
    def _():
        send(ar, ar, c1_s.at[0], c1_r, 0, 0).wait_recv()

    def across(q):
        @pl.when(c != 1)
        def _():
            send(ar.at[q, core], ar.at[q, core], c3_s.at[q], c3_r.at[q], r, sibling).start()

    @pl.when((c > 0) & (r > 0))
    def _():
        send(ar.at[h, core], ar.at[h, core], c1_s.at[0], c1_r, r, 0).wait_recv()

        def spread(d):
            q = lax.rem(h + d, 8)

            @pl.when((q != 0) | (core != 0))
            def _():
                send(
                    ar.at[h, core], ar.at[h, core], c2_s.at[q], c2_r.at[h], r, 2 * q + core
                ).start()

        each(1, 8, spread)
        across(h)

        def collect(d):
            q = lax.rem(h + d, 8)
            send(
                ar.at[q, core], ar.at[q, core], c2_s.at[q], c2_r.at[q], r, 2 * q + core
            ).wait_recv()
            across(q)

        each(1, 8, collect)
        each(0, 8, lambda q: send(
            ar.at[q, 1 - core], ar.at[q, 1 - core], c3_s.at[q], c3_r.at[q], r, sibling
        ).wait_recv())

    @pl.when(c > 0)
    def _():
        @pl.when(r >= h)
        def _():
            move(ar, ar_out, 3).start()

        @pl.when(r == h)
        def _():
            move(ar.at[pl.ds(4 * core, 4)], ac_out, 4).start()

            def scatter(d):
                q = lax.rem(r + d, NR)
                send(
                    ar.at[4 * core + q // 2, lax.rem(q, 2)], ac.at[q // 2, lax.rem(q, 2)],
                    d1_s.at[q], d1_r, q, c,
                ).start()

            each(1, NR, scatter)
            each(r + 1, NR, lambda q: send(
                ar.at[4 * core + r // 2, lax.rem(r, 2)], ac.at[r // 2, lax.rem(r, 2)],
                d2_s.at[q], d2_r.at[r], q, c,
            ).start())

        @pl.when(r != h)
        def _():
            mine = ac.at[r // 2, lax.rem(r, 2)]
            send(mine, mine, d1_s.at[0], d1_r, h, c).wait_recv()

            def on(q):
                @pl.when(q != r)
                def _():
                    send(mine, mine, d2_s.at[q], d2_r.at[r], q, c).start()

            each(h + 1, NR, on)

        send(xb.at[r], xb.at[r], x2_s.at[0], x2_r, r, 0).wait_recv()
        each(1, NR, lambda d: send(
            xb.at[r], xb.at[r], x3_s.at[lax.rem(r + d, NR)], x3_r.at[r], lax.rem(r + d, NR), c
        ).start())

        @pl.when(r > h)
        def _():
            def arrive(q):
                @pl.when(q != r)
                def _():
                    at = ac.at[q // 2, lax.rem(q, 2)]
                    send(at, at, d2_s.at[q], d2_r.at[q], q, c).wait_recv()

            each(0, NR, arrive)
            move(ac, ac_out, 4).start()

        @pl.when(r >= h)
        def _():
            def arrive(q):
                @pl.when(q != r)
                def _():
                    send(
                        wide_kids.at[pl.ds(0, 8)], kids.at[q], e2_s.at[0], e2_r.at[q], q, c
                    ).wait_recv()

            each(0, NR, arrive)

        def pieces(q):
            @pl.when(q != r)
            def _():
                send(xb.at[q], xb.at[q], x3_s.at[q], x3_r.at[q], q, c).wait_recv()

        each(0, NR, pieces)
        move(xb, xb_out, 1).start()

    @pl.when(c == 0)
    def _():
        def pieces(q):
            @pl.when((q != r) & (r > 0))
            def _():
                send(x3.at[q], x3.at[q], x3_s.at[q], x3_r.at[q], q, c).wait_recv()

        each(0, NR, pieces)
        move(x3, x3_out, 1).start()

    def sent(buffer, sem):
        send(buffer, buffer, sem, c1_r, r, sibling).wait_send()

    def unless(condition, body):
        pl.when(jnp.logical_not(condition))(body)

    @pl.when(c < 2)
    def _():
        unless(root, lambda: sent(turned.at[pl.ds(0, 2)], k_s))
        each(0, NR, lambda q: when(
            (q != r) | (c == 1), lambda: sent(bs.at[q], b_s.at[q])
        ))

    each(1, NC, lambda q: when(
        (q <= h + 8) & (q != c), lambda: sent(e1s.at[q], e1_s.at[q])
    ))

    @pl.when(c == 0)
    def _():
        move(pf, panel, 0).wait()
        move(x3, x3_out, 1).wait()

        @pl.when(r == 0)
        def _():
            sent(ar, c1_s.at[1])
            each(1, NR, lambda q: sent(x3.at[q], x1_s.at[q]))

        @pl.when(r > 0)
        def _():
            each(1, NC, lambda q: sent(ar.at[0, 0], c1_s.at[q]))
            each(1, 8, lambda q: sent(ar.at[0, 0], c2_s.at[q]))
            each(0, 8, lambda q: sent(ar.at[q, 0], c3_s.at[q]))

        each(1, NC, lambda q: sent(xb.at[0], x2_s.at[q]))
        each(1, NR, lambda q: when(q != r, lambda: sent(x3.at[0], x3_s.at[q])))

    @pl.when(c > 0)
    def _():
        def left_row(q):
            when(q != r, lambda: sent(wide_kids.at[pl.ds(8 * q, 8)], e2_s.at[q]))
            when(q == r, lambda: move(wide_kids.at[pl.ds(8 * q, 8)], kids.at[r], 2).wait())

        each(h, NR, left_row)

        @pl.when(r > 0)
        def _():
            each(0, 8, lambda q: when(
                (q != h) & ((q != 0) | (core != 0)), lambda: sent(ar.at[0, 0], c2_s.at[q])
            ))
            when(c != 1, lambda: each(0, 8, lambda q: sent(ar.at[0, 0], c3_s.at[q])))

        each(1, NR, lambda d: sent(xb.at[0], x3_s.at[lax.rem(r + d, NR)]))
        move(xb, xb_out, 1).wait()

        @pl.when(r >= h)
        def _():
            move(ar, ar_out, 3).wait()
            move(ac, ac_out, 4).wait()

        @pl.when(r == h)
        def _():
            each(1, NR, lambda d: sent(ar.at[0, 0], d1_s.at[lax.rem(r + d, NR)]))
            each(r + 1, NR, lambda q: sent(ar.at[0, 0], d2_s.at[q]))

        when(r != h, lambda: each(h + 1, NR, lambda q: when(
            q != r, lambda: sent(ac.at[0, 0], d2_s.at[q])
        )))


def ORDER(d):
    return d


def exchange(tab, fm, child, front):
    dma = pltpu.SemaphoreType.DMA
    sds = jax.ShapeDtypeStruct
    return pl.pallas_call(
        exchange_kernel,
        in_specs=[SM, SM, VM, ANY],
        out_specs=[ANY] * 6,
        out_shape=[
            sds((NR, 8, BS, BS), bf16),
            sds((8, 2, 128, 1024), bf16),
            sds((4, 2, 128, 1024), bf16),
            sds((8, 3, 64, 512), bf16),
            sds((8, 3, 64, 512), f32),
            sds((8, BS, 1024), f32),
        ],
        scratch_shapes=[
            pltpu.VMEM((16, BS, BS), bf16),
            pltpu.VMEM((16, BS, BS), bf16),
            pltpu.VMEM((NC, 2, BS, BS), bf16),
            pltpu.VMEM((NC, 2, BS, BS), bf16),
            pltpu.VMEM((64, BS, BS), bf16),
            pltpu.VMEM((NR, 4, BS, BS), bf16),
            pltpu.VMEM((8, BS, 1024), f32),
            pltpu.VMEM((8, 2, 128, 1024), bf16),
            pltpu.VMEM((4, 2, 128, 1024), bf16),
            pltpu.VMEM((8, 3, 64, 512), f32),
            pltpu.VMEM((8, 3, 64, 512), bf16),
            pltpu.VMEM((512, 1536), f32),
            pltpu.VMEM((128, 256), f32),
            pltpu.VMEM((128, 1536), f32),
            dma, dma((16,)),
            dma((NC,)), dma((NC,)), dma((NR,)), dma((NR,)), dma((NR,)), dma((16,)),
            dma((NC,)), dma, dma((8,)), dma((8,)), dma((8,)), dma((8,)),
            dma((NR,)), dma, dma((NR,)), dma((NR,)),
            dma((NR,)), dma, dma((NC,)), dma, dma((NR,)), dma((NR,)), dma((5,)),
        ],
        compiler_params=pltpu.CompilerParams(
            collective_id=1, has_side_effects=True, vmem_limit_bytes=56 << 20
        ),
        cost_estimate=pl.CostEstimate(flops=0, bytes_accessed=400_000_000, transcendentals=0),
        name="exchange",
    )(tab, fm, child, front)


def split(x):
    high = x.astype(bf16)
    return high, (x - high.astype(f32)).astype(bf16)


def update_kernel(
    tab, fm, front, panel, ar, ac, xb, x3, kids, out, inv0, low, inv1, low0, low1, low2, wc,
):
    r = lax.axis_index("row")
    c = lax.axis_index("col")
    i = pl.program_id(0)
    g = 8 * r + i
    active = g >= 4 * c

    def gather(ref, n):
        return jnp.concatenate([ref[p, n] for p in range(8)], axis=0)

    def solve(rows0, rows1, block_row):
        first = dot_t(rows0, inv0[...], None).astype(bf16)
        across = dot(first, low[...], None)
        second = jnp.concatenate(
            [
                rows1[:, BS * j : BS * j + BS].astype(f32)
                - fm[block_row, 2 + j].astype(f32) * across[:, BS * j : BS * j + BS]
                for j in range(2)
            ],
            axis=1,
        ).astype(bf16)
        return first, dot_t(second, inv1[...], None).astype(bf16)

    def thrice(product, x, high, rest):
        a, b = split(x)
        return (
            product(a, high[...], None) + product(a, rest[...], None) + product(b, high[...], None)
        )

    @pl.when((i == 0) & (c > 0) & (c // 2 <= r))
    def _():
        inv0[...] = gather(xb, 0)
        low[...] = gather(xb, 1)
        inv1[...] = gather(xb, 2)
        for j in range(4):
            block = jnp.concatenate([ac[j, 0], ac[j, 1]], axis=0)
            first, second = solve(block[:, :512], block[:, 512:], 4 * c + j)
            wc[BS * j : BS * j + BS, :512] = first
            wc[BS * j : BS * j + BS, 512:] = second

    @pl.when((i == 0) & (c == 0))
    def _():
        for n, (high, rest) in enumerate(((inv0, low0), (low, low1), (inv1, low2))):
            high[...], rest[...] = split(gather(x3, n))

    @pl.when(jnp.logical_not(active))
    def _():
        out[...] = jnp.zeros_like(out)

    @pl.when(active & (c == 0))
    def _():
        first = thrice(dot_t, panel[0, :, :512], inv0, low0)
        across = thrice(dot, first, low, low1)
        second = jnp.concatenate(
            [
                panel[0, :, 512 + BS * j : 768 + BS * j]
                - fm[g, 2 + j].astype(f32) * across[:, BS * j : BS * j + BS]
                for j in range(2)
            ],
            axis=1,
        )
        second = thrice(dot_t, second, inv1, low2)
        row = g * BS + lax.broadcasted_iota(jnp.int32, (BS, 512), 0)
        lane = lax.broadcasted_iota(jnp.int32, (BS, 512), 1)
        out[:, :512] = jnp.where(row >= lane, first, 0.0)
        out[:, 512:] = jnp.where(row >= lane + 512, second, 0.0)

    @pl.when(active & (c > 0))
    def _():
        block = jnp.concatenate([ar[0, 0], ar[0, 1]], axis=0)
        first, second = solve(block[:, :512], block[:, 512:], g)
        for j in range(4):
            at = pl.ds(BS * j, BS)
            keep = (fm[g, 4 * c + j] != 0) & (g >= 4 * c + j)

            @pl.when(keep)
            def _():
                product = dot_t(first, wc[BS * j : BS * j + BS, :512], None) + dot_t(
                    second, wc[BS * j : BS * j + BS, 512:], None
                )
                times = fm[g, 4 * c + j].astype(f32)
                out[:, at] = (front[:, at] - product) * times

                for k in range(NR):
                    slot = tab[24 + 8 * k + i]
                    side = tab[88 + 4 * k + j]

                    @pl.when(tab[120 + 8 * k + i] * tab[184 + 4 * k + j] > 0)
                    def _():
                        out[:, at] = out[:, at] + times * kids[k, 4 * side + slot].astype(f32)

            @pl.when(jnp.logical_not(keep))
            def _():
                out[:, at] = jnp.zeros((BS, BS), f32)


def update(tab, fm, front, panel, ar, ac, xb, x3, kids):
    whole = lambda shape: pl.BlockSpec(
        shape, lambda i: (0,) * len(shape), pipeline_mode=pl.Buffered(1)
    )
    return pl.pallas_call(
        update_kernel,
        grid=(8,),
        in_specs=[
            SM, SM,
            pl.BlockSpec((BS, 1024), lambda i: (i, 0)),
            pl.BlockSpec((1, BS, 1024), lambda i: (i, 0, 0)),
            pl.BlockSpec((1, 2, 128, 1024), lambda i: (i, 0, 0, 0)),
            whole((4, 2, 128, 1024)),
            whole((8, 3, 64, 512)),
            whole((8, 3, 64, 512)),
            whole((NR, 8, BS, BS)),
        ],
        out_specs=pl.BlockSpec((BS, 1024), lambda i: (i, 0)),
        out_shape=jax.ShapeDtypeStruct((2048, 1024), f32),
        scratch_shapes=[pltpu.VMEM((512, 512), bf16)] * 6 + [pltpu.VMEM((1024, 1024), bf16)],
        compiler_params=pltpu.CompilerParams(vmem_limit_bytes=48 << 20),
        name="update",
    )(tab, fm, front, panel, ar, ac, xb, x3, kids)


def tables(maps, r, c):
    own = lax.dynamic_index_in_dim(maps, r, 0, keepdims=False)
    row_start = jnp.minimum(jnp.sum(own[:, None] < 8 * jnp.arange(NR), axis=0), 12)
    col_start = jnp.minimum(jnp.sum(own[:, None] < 4 * jnp.arange(NC), axis=0), 14)
    index = jnp.arange(16)
    rows = maps[:, None, :] == 8 * r + jnp.arange(8)[None, :, None]
    row_first = jnp.minimum(jnp.sum(maps < 8 * r, axis=1), 12)
    row_slot = jnp.sum(rows * (index - row_first[:, None, None] + 1), axis=-1) - 1
    cols = maps[:, None, :] == 4 * c + jnp.arange(4)[None, :, None]
    col_first = jnp.minimum(jnp.sum(maps < 4 * c, axis=1), 14)
    col_slot = jnp.sum(cols * (index - col_first[:, None, None] + 1), axis=-1) - 1
    parts = [
        row_start,
        col_start,
        jnp.maximum(row_slot, 0).reshape(-1),
        jnp.maximum(col_slot, 0).reshape(-1),
        (row_slot >= 0).reshape(-1),
        (col_slot >= 0).reshape(-1),
    ]
    return jnp.concatenate([part.astype(jnp.int32) for part in parts])


def local(front, child_updates, child_maps, fill_mask):
    r = lax.axis_index("row")
    c = lax.axis_index("col")
    tab = tables(child_maps, r, c)
    kids, ar, ac, xb, x3, panel = exchange(
        tab, fill_mask, child_updates[0], front.reshape(8, BS, 1024)
    )
    return update(tab, fill_mask, front, panel, ar, ac, xb, x3, kids)


def solution(mesh):
    placed = (P("row", "col"), P("row", "col", None), P(), P())
    return jax.shard_map(
        local, mesh=mesh, in_specs=placed, out_specs=P("row", "col"), check_vma=False
    )
```

time: 391 us -> 319 us (0.82)
  the two profiles are of different devices: /device:TPU:1 before, /device:TPU:54 now
where the time goes in v2:
time: 319 us
  Pallas kernels  311 us (97%)
  local copies, waits for them, and re-layouts  4.83 us (2%)
    pallas_call x1, Pallas kernels, exchange(): pl.pallas_call(exchange_kernel, in_specs=[SM, SM, VM, ANY], out_specs=[AN...  287 us
    pallas_call x1, Pallas kernels, update(): pl.pallas_call(update_kernel, grid=(8,), in_specs=[SM, SM, pl.BlockSpec((...  23.8 us

profile of v2, /device:TPU:54, one launch (start us, length us, event | category | flops | bytes accessed | tf_op | source)
XLA Modules:
  0.0 318.9 jit_solution(1816555491895545960)
XLA Ops:
  0.0 0.7 dynamic-slice_bitcast_fusion
  0.7 0.8 convert_reduce_fusion.1
  1.6 0.2 convert_reduce_fusion.3
  1.8 0.1 convert_reduce_fusion
  1.8 0.1 subtract_add_fusion
  1.9 0.9 select_reduce_fusion.1
  2.8 0.1 copy.5
  2.9 0.1 max.17
  3.0 0.1 copy.6
  3.1 0.1 reshape.104
  3.2 0.1 subtract_add_fusion.1
  3.2 1.0 select_reduce_fusion
  4.2 0.1 reshape.103
  4.3 0.1 max.15
  4.4 0.7 concatenate.3.tab
  5.1 0.0 copy-start.2
  5.1 0.0 copy-start.3
  5.1 287.0 %exchange.1 = (bf16[8,8,256,256]{3,2,1,0:T(8,128)(2,1)}, bf16[8,2,128,1024]{3,2,1,0:T(8,128)(2,1)}, bf16[4,2,128,1024]{3,2,1,0:T(8,128)(2,1)}, bf16[8,3,64,512]{...) custom-call(s32[216]{0:T(256)} %concatenate.3.tab, s32[64,64]{1,0:T(8,128)} %fm.3, ...), custom_call_target="tpu_custom_call" | custom-call | bytes 400000000 | tf_op jit(solution)/shard_map/exchange/pallas_call | solution.py:590
  292.1 0.0 copy-done.2
  292.1 0.0 copy-done.3
  292.1 0.0 copy-start
  292.1 1.6 copy-done
  293.7 0.0 copy-start.1
  293.7 1.4 copy-done.1
  295.1 23.8 %update.1 = f32[2048,1024]{1,0:T(8,128)} custom-call(s32[216]{0:T(256)S(1)} %copy-done.3, s32[64,64]{1,0:T(8,128)S(1)} %copy-done.2, f32[2048,1024]{1,0:T(8,128)} %front.1, f32[8,256,1024]{2,1,0:T(8,128)} %get-tuple-element.11.panel, bf16[8,2,128,1024]{3,2,1,0:T(8,128)(2,1)} %get-tuple-element.12.ar, bf16[4,2,128,1024]{3,2,1,0:T(8,128)(2,1)S(1)} %copy-done, ...), custom_call_target="tpu_custom_call" | custom-call | tf_op jit(solution)/shard_map/update/pallas_call | solution.py:738
  (11 shorter events, 0.1 us)
Async XLA Ops:
  5.1 287.0 %copy-start.2 = (s32[64,64]{1,0:T(8,128)S(1)}, s32[64,64]{1,0:T(8,128)}, u32[]{:S(2)}) copy-start(s32[64,64]{1,0:T(8,128)} %fm.3) | copy-start | bytes 49156
  5.1 287.0 %copy-start.3 = (s32[216]{0:T(256)S(1)}, s32[216]{0:T(256)}, u32[]{:S(2)}) copy-start(s32[216]{0:T(256)} %concatenate.3.tab) | copy-start | bytes 2596
  292.1 1.6 copy-start
  293.7 1.4 copy-start.1

commit v3 on v2

--- a/solution.py
+++ b/solution.py
@@ -162,15 +162,19 @@
 
 def exchange_kernel(
     tab, fm, child, front, kids, ar_out, ac_out, xb_out, x3_out, panel,
-    blocks, turned, e1s, e1r, wide_kids, bs, pf, ar, ac, x3, xb, wide, small, r_ref,
+    blocks, turned, corners, e1s, e1r_0, e1r_1, wide_kids, bs, pf, ar, ac, x3, xb, wide, small, r_ref,
     k_s, k_r, e1_s, e1_r, e2_s, e2_r, b_s, b_r, c1_s, c1_r, c2_s, c2_r, c3_s, c3_r,
-    d1_s, d1_r, d2_s, d2_r, x1_s, x1_r, x2_s, x2_r, x3_s, x3_r, here,
+    d1_s, d1_r, d2_s, d2_r, dz_s, dz_r, x1_s, x1_r, x2_s, x2_r, x3_s, x3_r, here,
 ):
     r = lax.axis_index("row")
     c = lax.axis_index("col")
     h = c // 2
     core = lax.rem(c, 2)
     sibling = c + 1 - 2 * core
+    e1r = (e1r_0, e1r_1)
+    z = r // 4
+    y = lax.rem(r, 4)
+    partner = lax.rem(r + 4, NR)
     root = (r == 0) & (c == 0)
     barrier = pltpu.get_barrier_semaphore()
 
@@ -219,12 +223,12 @@
 
     @pl.when((c < 2) & jnp.logical_not(root))
     def _():
-        send(turned.at[pl.ds(0, 2)], e1r.at[2 * r + c], k_s, k_r.at[2 * r + c], 0, 0).start()
+        send(turned.at[pl.ds(0, 2)], corners.at[2 * r + c], k_s, k_r.at[2 * r + c], 0, 0).start()
 
     @pl.when(root)
     def _():
         for n in range(2):
-            e1r[0, n] = turned[n]
+            corners[0, n] = turned[n]
 
     @pl.when(c < 2)
     def _():
@@ -247,23 +251,35 @@
 
         each(1, NR + 1, give)
 
-    def to_col(d):
-        q = lax.rem(c + d, NC)
-
-        @pl.when((q >= 1) & (q <= h + 8))
-        def _():
-            @pl.when(q != c)
-            def _():
-                for n in range(2):
-                    e1s[q, n] = blocks[tab[8 + q] + n]
-                send(e1s.at[q], e1r.at[c], e1_s.at[q], e1_r.at[c], r, q).start()
-
-            @pl.when(q == c)
-            def _():
-                for n in range(2):
-                    e1r[c, n] = blocks[tab[8 + q] + n]
-
-    each(1, NC + 1, to_col)
+    def to_col(m):
+        def run(d):
+            q = lax.rem(c + d, NC)
+
+            @pl.when((q >= 1) & (q <= h + 8))
+            def _():
+                @pl.when(q != c)
+                def _():
+                    e1s[q, m] = blocks[tab[8 + q] + m]
+                    send(
+                        e1s.at[q, m], e1r[m].at[c], e1_s.at[16 * m + q], e1_r.at[16 * m + c], r, q
+                    ).start()
+
+                @pl.when(q == c)
+                def _():
+                    e1r[m][c] = blocks[tab[8 + q] + m]
+
+        each(1, NC + 1, run)
+
+    def left_col(m):
+        each(1, NC, lambda q: when(
+            (q <= h + 8) & (q != c), lambda: sent(e1s.at[q, m], e1_s.at[16 * m + q])
+        ))
+
+    def sent(buffer, sem):
+        send(buffer, buffer, sem, c1_r, r, sibling).wait_send()
+
+    to_col(0)
+    when(c == 0, lambda: to_col(1))
 
     def assemble_panel():
         move(front.at[pl.ds(0, 4)], pf.at[pl.ds(0, 4)], 3).wait()
@@ -279,63 +295,84 @@
         each(0, 16, arrive)
 
         def assemble(i):
-            def add(k):
-                for j in range(4):
-                    times = (tab[120 + 8 * k + i] * tab[184 + 4 * k + j]).astype(f32)
-                    block = wide_kids[8 * k + 4 * tab[88 + 4 * k + j] + tab[24 + 8 * k + i]]
-                    at = pl.ds(j * BS, BS)
-                    pf[i, :, at] = pf[i, :, at] + times * block.astype(f32)
-
-            each(0, NR, add)
             for j in range(4):
                 at = pl.ds(j * BS, BS)
-                kept = pf[i, :, at] * fm[8 * r + i, j].astype(f32)
-                pf[i, :, at] = kept
-                ar[i, 0, :, at] = kept[:128].astype(bf16)
-                ar[i, 1, :, at] = kept[128:].astype(bf16)
+                keep = fm[8 * r + i, j].astype(f32)
+                pairs = []
+                for k in range(NR):
+                    pairs.append((
+                        (tab[120 + 8 * k + i] * tab[184 + 4 * k + j]).astype(f32),
+                        8 * k + 4 * tab[88 + 4 * k + j] + tab[24 + 8 * k + i],
+                    ))
+                for n in range(4):
+                    low = 64 * n
+                    total = pf[i, low : low + 64, at]
+                    for times, from_slot in pairs:
+                        total = total + times * wide_kids[from_slot, low : low + 64, :].astype(f32)
+                    total = total * keep
+                    pf[i, low : low + 64, at] = total
+                    ar[i, n // 2, low % 128 : low % 128 + 64, at] = total.astype(bf16)
 
         each(0, 8, assemble)
         move(pf, panel, 0).start()
 
+    def part(ref, q, t):
+        return ref.at[q, pl.ds(2 * t, 2 - t)]
+
+    def pivots_from_root(t):
+        each(1, NR, lambda q: send(
+            part(x3, q, t), part(x3, q, t), x1_s.at[8 * t + q], x1_r.at[t], q, 0
+        ).start())
+
+    def pivots_out(t):
+        for n in ((0, 1), (2,))[t]:
+            xb[r, n] = x3[r, n].astype(bf16)
+        each(1, NC, lambda q: send(
+            part(xb, r, t), part(xb, r, t), x2_s.at[16 * t + q], x2_r.at[t], r, q
+        ).start())
+        each(1, NR, lambda q: when(q != r, lambda: send(
+            part(x3, r, t), part(x3, r, t), x3_s.at[12 * t + q], x3_r.at[8 * t + r], q, 0
+        ).start()))
+
     @pl.when(root)
     def _():
         move(front.at[pl.ds(0, 4)], pf.at[pl.ds(0, 4)], 0).wait()
         each(1, 16, lambda k: send(
-            turned.at[pl.ds(0, 2)], e1r.at[k], k_s, k_r.at[k], k // 2, lax.rem(k, 2)
+            turned.at[pl.ds(0, 2)], corners.at[k], k_s, k_r.at[k], k // 2, lax.rem(k, 2)
         ).wait_recv())
         for n, rows, cols in ((0, 0, 0), (1, 0, 2), (2, 2, 2)):
-            for i in range(2):
+
+            def corner(i):
                 for j in range(2):
+                    keep = fm[rows + i, cols + j].astype(f32)
+                    pairs = []
+                    for k in range(NR):
+                        pairs.append((
+                            (tab[120 + 8 * k + rows + i] * tab[184 + 4 * k + cols + j]).astype(f32),
+                            2 * k + tab[88 + 4 * k + cols + j],
+                            tab[24 + 8 * k + rows + i],
+                        ))
                     for p in range(4):
-                        x3[4 * i + p, n, :, BS * j : BS * j + BS] = pf[
+                        total = pf[
                             rows + i, 64 * p : 64 * p + 64,
                             BS * (cols + j) : BS * (cols + j) + BS,
                         ]
-
-                    def add(k):
-                        times = (
-                            tab[120 + 8 * k + rows + i] * tab[184 + 4 * k + cols + j]
-                        ).astype(f32)
-                        block = e1r[
-                            2 * k + tab[88 + 4 * k + cols + j], tab[24 + 8 * k + rows + i]
-                        ].astype(f32) * times
-                        for p in range(4):
-                            at = pl.ds(BS * j, BS)
-                            x3[4 * i + p, n, :, at] = (
-                                x3[4 * i + p, n, :, at] + block[64 * p : 64 * p + 64]
-                            )
-
-                    each(0, NR, add)
-                    keep = fm[rows + i, cols + j].astype(f32)
-                    for p in range(4):
-                        at = pl.ds(BS * j, BS)
-                        x3[4 * i + p, n, :, at] = x3[4 * i + p, n, :, at] * keep
+                        for times, side, slot in pairs:
+                            total = total + times * corners[
+                                side, slot, 64 * p : 64 * p + 64, :
+                            ].astype(f32)
+                        x3[4 * i + p, n, :, BS * j : BS * j + BS] = total * keep
+
+            each(0, 2, corner)
         first_pivot(x3, wide, small, r_ref)
+        pivots_from_root(0)
+        pivots_out(0)
         second_matrix(x3, fm, wide)
         assemble_panel()
         send(ar, ar, c1_s.at[1], c1_r, 0, 1).start()
         second_pivot(x3, wide, small, r_ref)
-        each(1, NR, lambda q: send(x3.at[q], x3.at[q], x1_s.at[q], x1_r, q, 0).start())
+        pivots_from_root(1)
+        pivots_out(1)
 
     @pl.when((c == 0) & (r > 0))
     def _():
@@ -350,49 +387,47 @@
         each(0, 8, lambda q: send(
             ar.at[q, 0], ar.at[q, 0], c3_s.at[q], c3_r.at[q], r, 1
         ).start())
-        send(x3.at[r], x3.at[r], x1_s.at[0], x1_r, 0, 0).wait_recv()
-
-    @pl.when(c == 0)
-    def _():
-        xb[r] = x3[r].astype(bf16)
-        each(1, NC, lambda q: send(xb.at[r], xb.at[r], x2_s.at[q], x2_r, r, q).start())
-
-        def on(q):
-            @pl.when(q != r)
-            def _():
-                send(x3.at[r], x3.at[r], x3_s.at[q], x3_r.at[r], q, 0).start()
-
-        each(1, NR, on)
-
-    @pl.when(c > 0)
-    def _():
+        for t in range(2):
+            send(part(x3, r, t), part(x3, r, t), x1_s.at[0], x1_r.at[t], 0, 0).wait_recv()
+            pivots_out(t)
+
+    def to_row(m):
         def arrive(a):
             @pl.when(a != c)
             def _():
-                send(e1s.at[0], e1r.at[a], e1_s.at[0], e1_r.at[a], r, a).wait_recv()
+                send(
+                    e1s.at[0, m], e1r[m].at[a], e1_s.at[0], e1_r.at[16 * m + a], r, a
+                ).wait_recv()
 
         each(jnp.maximum(2 * (c - 8), 0), NC, arrive)
 
-        def to_row(d):
-            q = lax.rem(r + ORDER(d), NR)
+        def run(d):
+            q = lax.rem(r + d, NR)
+            mine = wide_kids.at[pl.ds(8 * q + 4 * m, 4)]
+            there = kids.at[r, pl.ds(4 * m, 4)]
 
             @pl.when(q >= h)
             def _():
                 for n in range(4):
-                    for m in range(2):
-                        wide_kids[8 * q + 4 * m + n] = e1r[tab[q] + n, m]
+                    wide_kids[8 * q + 4 * m + n] = e1r[m][tab[q] + n]
 
                 @pl.when(q != r)
                 def _():
-                    send(
-                        wide_kids.at[pl.ds(8 * q, 8)], kids.at[r], e2_s.at[q], e2_r.at[r], q, c
-                    ).start()
+                    send(mine, there, e2_s.at[8 * m + q], e2_r.at[8 * m + r], q, c).start()
 
                 @pl.when(q == r)
                 def _():
-                    move(wide_kids.at[pl.ds(8 * q, 8)], kids.at[r], 2).start()
-
-        each(1, NR + 1, to_row)
+                    move(mine, there, 5 + m).start()
+
+        for d in (4, 5, 6, 7, 1, 3, 2, 8):
+            run(d)
+
+    @pl.when(c > 0)
+    def _():
+        left_col(0)
+        to_col(1)
+        to_row(0)
+        to_row(1)
 
     @pl.when((r == 0) & (c == 1))
     def _():
@@ -437,66 +472,90 @@
         def _():
             move(ar, ar_out, 3).start()
 
+        def match_along(piece):
+            def on(d):
+                q = 4 * z + lax.rem(y + d, 4)
+
+                @pl.when(q > h)
+                def _():
+                    send(piece, ac.at[y], d2_s.at[lax.rem(q, 4)], d2_r.at[y], q, c).start()
+
+            each(1, 4, on)
+
+        def match_on(piece):
+            @pl.when(z == 0)
+            def _():
+                send(piece, ac.at[y], dz_s, dz_r, partner, c).start()
+
+            match_along(piece)
+
         @pl.when(r == h)
         def _():
             move(ar.at[pl.ds(4 * core, 4)], ac_out, 4).start()
 
-            def scatter(d):
-                q = lax.rem(r + d, NR)
-                send(
-                    ar.at[4 * core + q // 2, lax.rem(q, 2)], ac.at[q // 2, lax.rem(q, 2)],
-                    d1_s.at[q], d1_r, q, c,
-                ).start()
-
-            each(1, NR, scatter)
-            each(r + 1, NR, lambda q: send(
-                ar.at[4 * core + r // 2, lax.rem(r, 2)], ac.at[r // 2, lax.rem(r, 2)],
-                d2_s.at[q], d2_r.at[r], q, c,
+            each(1, 4, lambda d: send(
+                ar.at[4 * core + lax.rem(y + d, 4)], ac.at[lax.rem(y + d, 4)],
+                d1_s.at[lax.rem(y + d, 4)], d1_r, 4 * z + lax.rem(y + d, 4), c,
             ).start())
-
-        @pl.when(r != h)
-        def _():
-            mine = ac.at[r // 2, lax.rem(r, 2)]
-            send(mine, mine, d1_s.at[0], d1_r, h, c).wait_recv()
-
-            def on(q):
-                @pl.when(q != r)
-                def _():
-                    send(mine, mine, d2_s.at[q], d2_r.at[r], q, c).start()
-
-            each(h + 1, NR, on)
-
-        send(xb.at[r], xb.at[r], x2_s.at[0], x2_r, r, 0).wait_recv()
-        each(1, NR, lambda d: send(
-            xb.at[r], xb.at[r], x3_s.at[lax.rem(r + d, NR)], x3_r.at[r], lax.rem(r + d, NR), c
-        ).start())
+            match_on(ar.at[4 * core + y])
+
+        @pl.when((r != h) & (z == h // 4))
+        def _():
+            send(ac.at[y], ac.at[y], d1_s.at[0], d1_r, h, c).wait_recv()
+            match_on(ac.at[y])
+
+        @pl.when(z > h // 4)
+        def _():
+            send(ac.at[y], ac.at[y], dz_s, dz_r, partner, c).wait_recv()
+            match_along(ac.at[y])
+
+        def pivots_along(p, t, base):
+            each(1, 4, lambda d: send(
+                part(xb, p, t), part(xb, p, t), x3_s.at[12 * t + base + lax.rem(y + d, 4)],
+                x3_r.at[8 * t + p], 4 * z + lax.rem(y + d, 4), c,
+            ).start())
+
+        for t in range(2):
+            send(part(xb, r, t), part(xb, r, t), x2_s.at[0], x2_r.at[t], r, 0).wait_recv()
+            send(
+                part(xb, r, t), part(xb, r, t),
+                x3_s.at[12 * t + partner], x3_r.at[8 * t + r], partner, c,
+            ).start()
+            pivots_along(r, t, 4 * z)
+            send(
+                part(xb, partner, t), part(xb, partner, t),
+                x3_s.at[r], x3_r.at[8 * t + partner], partner, c,
+            ).wait_recv()
+            pivots_along(partner, t, 8)
 
         @pl.when(r > h)
+        def _():
+            each(1, 4, lambda d: send(
+                ac.at[lax.rem(y + d, 4)], ac.at[lax.rem(y + d, 4)],
+                d2_s.at[0], d2_r.at[lax.rem(y + d, 4)], 4 * z + lax.rem(y + d, 4), c,
+            ).wait_recv())
+            move(ac, ac_out, 4).start()
+
+        @pl.when(r >= h)
         def _():
             def arrive(q):
                 @pl.when(q != r)
                 def _():
-                    at = ac.at[q // 2, lax.rem(q, 2)]
-                    send(at, at, d2_s.at[q], d2_r.at[q], q, c).wait_recv()
+                    for m in range(2):
+                        send(
+                            wide_kids.at[pl.ds(0, 4)], kids.at[q, pl.ds(4 * m, 4)],
+                            e2_s.at[0], e2_r.at[8 * m + q], q, c,
+                        ).wait_recv()
 
             each(0, NR, arrive)
-            move(ac, ac_out, 4).start()
-
-        @pl.when(r >= h)
-        def _():
-            def arrive(q):
-                @pl.when(q != r)
-                def _():
+
+        def pieces(q):
+            @pl.when((q != r) & (q != partner))
+            def _():
+                for t in range(2):
                     send(
-                        wide_kids.at[pl.ds(0, 8)], kids.at[q], e2_s.at[0], e2_r.at[q], q, c
+                        part(xb, q, t), part(xb, q, t), x3_s.at[q], x3_r.at[8 * t + q], q, c
                     ).wait_recv()
-
-            each(0, NR, arrive)
-
-        def pieces(q):
-            @pl.when(q != r)
-            def _():
-                send(xb.at[q], xb.at[q], x3_s.at[q], x3_r.at[q], q, c).wait_recv()
 
         each(0, NR, pieces)
         move(xb, xb_out, 1).start()
@@ -506,13 +565,13 @@
         def pieces(q):
             @pl.when((q != r) & (r > 0))
             def _():
-                send(x3.at[q], x3.at[q], x3_s.at[q], x3_r.at[q], q, c).wait_recv()
+                for t in range(2):
+                    send(
+                        part(x3, q, t), part(x3, q, t), x3_s.at[q], x3_r.at[8 * t + q], q, c
+                    ).wait_recv()
 
         each(0, NR, pieces)
         move(x3, x3_out, 1).start()
-
-    def sent(buffer, sem):
-        send(buffer, buffer, sem, c1_r, r, sibling).wait_send()
 
     def unless(condition, body):
         pl.when(jnp.logical_not(condition))(body)
@@ -524,9 +583,8 @@
             (q != r) | (c == 1), lambda: sent(bs.at[q], b_s.at[q])
         ))
 
-    each(1, NC, lambda q: when(
-        (q <= h + 8) & (q != c), lambda: sent(e1s.at[q], e1_s.at[q])
-    ))
+    when(c == 0, lambda: left_col(0))
+    left_col(1)
 
     @pl.when(c == 0)
     def _():
@@ -536,7 +594,8 @@
         @pl.when(r == 0)
         def _():
             sent(ar, c1_s.at[1])
-            each(1, NR, lambda q: sent(x3.at[q], x1_s.at[q]))
+            for t in range(2):
+                each(1, NR, lambda q: sent(part(x3, q, t), x1_s.at[8 * t + q]))
 
         @pl.when(r > 0)
         def _():
@@ -544,14 +603,19 @@
             each(1, 8, lambda q: sent(ar.at[0, 0], c2_s.at[q]))
             each(0, 8, lambda q: sent(ar.at[q, 0], c3_s.at[q]))
 
-        each(1, NC, lambda q: sent(xb.at[0], x2_s.at[q]))
-        each(1, NR, lambda q: when(q != r, lambda: sent(x3.at[0], x3_s.at[q])))
+        for t in range(2):
+            each(1, NC, lambda q: sent(part(xb, 0, t), x2_s.at[16 * t + q]))
+            each(1, NR, lambda q: when(
+                q != r, lambda: sent(part(x3, 0, t), x3_s.at[12 * t + q])
+            ))
 
     @pl.when(c > 0)
     def _():
         def left_row(q):
-            when(q != r, lambda: sent(wide_kids.at[pl.ds(8 * q, 8)], e2_s.at[q]))
-            when(q == r, lambda: move(wide_kids.at[pl.ds(8 * q, 8)], kids.at[r], 2).wait())
+            for m in range(2):
+                mine = wide_kids.at[pl.ds(8 * q + 4 * m, 4)]
+                when(q != r, lambda: sent(mine, e2_s.at[8 * m + q]))
+                when(q == r, lambda: move(mine, kids.at[r, pl.ds(4 * m, 4)], 5 + m).wait())
 
         each(h, NR, left_row)
 
@@ -562,7 +626,12 @@
             ))
             when(c != 1, lambda: each(0, 8, lambda q: sent(ar.at[0, 0], c3_s.at[q])))
 
-        each(1, NR, lambda d: sent(xb.at[0], x3_s.at[lax.rem(r + d, NR)]))
+        for t in range(2):
+            sent(part(xb, 0, t), x3_s.at[12 * t + partner])
+            for base in (4 * z, 8):
+                each(1, 4, lambda d: sent(
+                    part(xb, 0, t), x3_s.at[12 * t + base + lax.rem(y + d, 4)]
+                ))
         move(xb, xb_out, 1).wait()
 
         @pl.when(r >= h)
@@ -570,18 +639,14 @@
             move(ar, ar_out, 3).wait()
             move(ac, ac_out, 4).wait()
 
-        @pl.when(r == h)
-        def _():
-            each(1, NR, lambda d: sent(ar.at[0, 0], d1_s.at[lax.rem(r + d, NR)]))
-            each(r + 1, NR, lambda q: sent(ar.at[0, 0], d2_s.at[q]))
-
-        when(r != h, lambda: each(h + 1, NR, lambda q: when(
-            q != r, lambda: sent(ac.at[0, 0], d2_s.at[q])
-        )))
-
-
-def ORDER(d):
-    return d
+        when(r == h, lambda: each(1, 4, lambda d: sent(ac.at[0], d1_s.at[lax.rem(y + d, 4)])))
+
+        @pl.when(z >= h // 4)
+        def _():
+            when((z == 0) & (h < 4), lambda: sent(ac.at[0], dz_s))
+            each(1, 4, lambda d: when(
+                4 * z + lax.rem(y + d, 4) > h, lambda: sent(ac.at[0], d2_s.at[lax.rem(y + d, 4)])
+            ))
 
 
 def exchange(tab, fm, child, front):
@@ -602,8 +667,10 @@
         scratch_shapes=[
             pltpu.VMEM((16, BS, BS), bf16),
             pltpu.VMEM((16, BS, BS), bf16),
+            pltpu.VMEM((16, 2, BS, BS), bf16),
             pltpu.VMEM((NC, 2, BS, BS), bf16),
-            pltpu.VMEM((NC, 2, BS, BS), bf16),
+            pltpu.VMEM((NC, BS, BS), bf16),
+            pltpu.VMEM((NC, BS, BS), bf16),
             pltpu.VMEM((64, BS, BS), bf16),
             pltpu.VMEM((NR, 4, BS, BS), bf16),
             pltpu.VMEM((8, BS, 1024), f32),
@@ -615,13 +682,14 @@
             pltpu.VMEM((128, 256), f32),
             pltpu.VMEM((128, 1536), f32),
             dma, dma((16,)),
-            dma((NC,)), dma((NC,)), dma((NR,)), dma((NR,)), dma((NR,)), dma((16,)),
+            dma((32,)), dma((32,)), dma((16,)), dma((16,)),
+            dma((NR,)), dma((16,)),
             dma((NC,)), dma, dma((8,)), dma((8,)), dma((8,)), dma((8,)),
-            dma((NR,)), dma, dma((NR,)), dma((NR,)),
-            dma((NR,)), dma, dma((NC,)), dma, dma((NR,)), dma((NR,)), dma((5,)),
+            dma((4,)), dma, dma((4,)), dma((4,)), dma, dma,
+            dma((16,)), dma((2,)), dma((32,)), dma((2,)), dma((24,)), dma((16,)), dma((7,)),
         ],
         compiler_params=pltpu.CompilerParams(
-            collective_id=1, has_side_effects=True, vmem_limit_bytes=56 << 20
+            collective_id=1, has_side_effects=True, vmem_limit_bytes=58 << 20
         ),
         cost_estimate=pl.CostEstimate(flops=0, bytes_accessed=400_000_000, transcendentals=0),
         name="exchange",

time: 319 us -> 293 us (0.918)
  the two profiles are of different devices: /device:TPU:54 before, /device:TPU:112 now
where the time goes in v3:
time: 293 us
  Pallas kernels  285 us (97%)
  local copies, waits for them, and re-layouts  4.83 us (2%)
  other arithmetic  3.16 us (1%)
    pallas_call x1, Pallas kernels, exchange(): pl.pallas_call(exchange_kernel, in_specs=[SM, SM, VM, ANY], out_specs=[AN...  260 us
    pallas_call x1, Pallas kernels, update(): pl.pallas_call(update_kernel, grid=(8,), in_specs=[SM, SM, pl.BlockSpec((...  25 us

profile of v3, /device:TPU:112, one launch (start us, length us, event | category | flops | bytes accessed | tf_op | source)
XLA Modules:
  0.0 292.7 jit_solution(11757580204429505052)
XLA Ops:
  0.0 0.7 dynamic-slice_bitcast_fusion
  0.7 0.8 convert_reduce_fusion.1
  1.6 0.2 convert_reduce_fusion.3
  1.8 0.1 convert_reduce_fusion
  1.8 0.1 subtract_add_fusion
  1.9 0.9 select_reduce_fusion.1
  2.8 0.1 copy.5
  2.9 0.1 max.17
  3.0 0.1 copy.6
  3.1 0.1 reshape.104
  3.2 0.1 subtract_add_fusion.1
  3.2 1.0 select_reduce_fusion
  4.2 0.1 reshape.103
  4.3 0.1 max.15
  4.4 0.7 concatenate.3.tab
  5.1 0.0 copy-start.2
  5.1 0.0 copy-start.3
  5.1 259.6 %exchange.1 = (bf16[8,8,256,256]{3,2,1,0:T(8,128)(2,1)}, bf16[8,2,128,1024]{3,2,1,0:T(8,128)(2,1)}, bf16[4,2,128,1024]{3,2,1,0:T(8,128)(2,1)}, bf16[8,3,64,512]{...) custom-call(s32[216]{0:T(256)} %concatenate.3.tab, s32[64,64]{1,0:T(8,128)} %fm.3, ...), custom_call_target="tpu_custom_call" | custom-call | bytes 400000000 | tf_op jit(solution)/shard_map/exchange/pallas_call | solution.py:655
  264.7 0.0 copy-done.2
  264.7 0.0 copy-done.3
  264.7 0.0 copy-start
  264.7 1.6 copy-done
  266.3 0.0 copy-start.1
  266.3 1.4 copy-done.1
  267.7 25.0 %update.1 = f32[2048,1024]{1,0:T(8,128)} custom-call(s32[216]{0:T(256)S(1)} %copy-done.3, s32[64,64]{1,0:T(8,128)S(1)} %copy-done.2, f32[2048,1024]{1,0:T(8,128)} %front.1, f32[8,256,1024]{2,1,0:T(8,128)} %get-tuple-element.11.panel, bf16[8,2,128,1024]{3,2,1,0:T(8,128)(2,1)} %get-tuple-element.12.ar, bf16[4,2,128,1024]{3,2,1,0:T(8,128)(2,1)S(1)} %copy-done, ...), custom_call_target="tpu_custom_call" | custom-call | tf_op jit(solution)/shard_map/update/pallas_call | solution.py:806
  (11 shorter events, 0.1 us)
Async XLA Ops:
  5.1 259.6 %copy-start.2 = (s32[64,64]{1,0:T(8,128)S(1)}, s32[64,64]{1,0:T(8,128)}, u32[]{:S(2)}) copy-start(s32[64,64]{1,0:T(8,128)} %fm.3) | copy-start | bytes 49156
  5.1 259.6 %copy-start.3 = (s32[216]{0:T(256)S(1)}, s32[216]{0:T(256)}, u32[]{:S(2)}) copy-start(s32[216]{0:T(256)} %concatenate.3.tab) | copy-start | bytes 2596
  264.7 1.6 copy-start
  266.3 1.4 copy-start.1

commit v4 on v3

--- a/solution.py
+++ b/solution.py
@@ -162,7 +162,7 @@
 
 def exchange_kernel(
     tab, fm, child, front, kids, ar_out, ac_out, xb_out, x3_out, panel,
-    blocks, turned, corners, e1s, e1r_0, e1r_1, wide_kids, bs, pf, ar, ac, x3, xb, wide, small, r_ref,
+    blocks, turned, corners, e1s, e1r_0, e1r_1, held_0, held_1, bs, pf, ar, ac, x3, xb, wide, small, r_ref,
     k_s, k_r, e1_s, e1_r, e2_s, e2_r, b_s, b_r, c1_s, c1_r, c2_s, c2_r, c3_s, c3_r,
     d1_s, d1_r, d2_s, d2_r, dz_s, dz_r, x1_s, x1_r, x2_s, x2_r, x3_s, x3_r, here,
 ):
@@ -172,6 +172,7 @@
     core = lax.rem(c, 2)
     sibling = c + 1 - 2 * core
     e1r = (e1r_0, e1r_1)
+    held = (held_0, held_1)
     z = r // 4
     y = lax.rem(r, 4)
     partner = lax.rem(r + 4, NR)
@@ -232,24 +233,25 @@
 
     @pl.when(c < 2)
     def _():
-        def give(d):
+        def give(t, d):
             q = lax.rem(r + d, NR)
             for n in range(4):
-                bs[q, n] = turned[tab[q] + n]
+                bs[t, q, n] = turned[tab[q] + n, 128 * t : 128 * t + 128, :]
 
             @pl.when((q != r) | (c == 1))
             def _():
                 send(
-                    bs.at[q], wide_kids.at[pl.ds(8 * r + 4 * c, 4)],
-                    b_s.at[q], b_r.at[2 * r + c], q, 0,
+                    bs.at[t, q], held[t].at[pl.ds(8 * r + 4 * c, 4)],
+                    b_s.at[8 * t + q], b_r.at[16 * t + 2 * r + c], q, 0,
                 ).start()
 
             @pl.when((q == r) & (c == 0))
             def _():
                 for n in range(4):
-                    wide_kids[8 * r + n] = bs[q, n]
-
-        each(1, NR + 1, give)
+                    held[t][8 * r + n] = bs[t, q, n]
+
+        for t in range(2):
+            each(1, NR + 1, functools.partial(give, t))
 
     def to_col(m):
         def run(d):
@@ -281,20 +283,18 @@
     to_col(0)
     when(c == 0, lambda: to_col(1))
 
-    def assemble_panel():
+    def assemble_panel(give_rows):
         move(front.at[pl.ds(0, 4)], pf.at[pl.ds(0, 4)], 3).wait()
 
-        def arrive(k):
+        def arrive(t, k):
             @pl.when(k != 2 * r)
             def _():
                 send(
-                    bs.at[0], wide_kids.at[pl.ds(4 * k, 4)],
-                    b_s.at[0], b_r.at[k], k // 2, lax.rem(k, 2),
+                    bs.at[0, 0], held[t].at[pl.ds(4 * k, 4)],
+                    b_s.at[0], b_r.at[16 * t + k], k // 2, lax.rem(k, 2),
                 ).wait_recv()
 
-        each(0, 16, arrive)
-
-        def assemble(i):
+        def assemble(t, i):
             for j in range(4):
                 at = pl.ds(j * BS, BS)
                 keep = fm[8 * r + i, j].astype(f32)
@@ -304,16 +304,21 @@
                         (tab[120 + 8 * k + i] * tab[184 + 4 * k + j]).astype(f32),
                         8 * k + 4 * tab[88 + 4 * k + j] + tab[24 + 8 * k + i],
                     ))
-                for n in range(4):
-                    low = 64 * n
+                for n in range(2):
+                    low = 128 * t + 64 * n
                     total = pf[i, low : low + 64, at]
                     for times, from_slot in pairs:
-                        total = total + times * wide_kids[from_slot, low : low + 64, :].astype(f32)
+                        total = total + times * held[t][
+                            from_slot, 64 * n : 64 * n + 64, :
+                        ].astype(f32)
                     total = total * keep
                     pf[i, low : low + 64, at] = total
-                    ar[i, n // 2, low % 128 : low % 128 + 64, at] = total.astype(bf16)
-
-        each(0, 8, assemble)
+                    ar[i, t, 64 * n : 64 * n + 64, at] = total.astype(bf16)
+            give_rows(t, i)
+
+        for t in range(2):
+            each(0, 16, functools.partial(arrive, t))
+            each(0, 8, functools.partial(assemble, t))
         move(pf, panel, 0).start()
 
     def part(ref, q, t):
@@ -368,8 +373,9 @@
         pivots_from_root(0)
         pivots_out(0)
         second_matrix(x3, fm, wide)
-        assemble_panel()
-        send(ar, ar, c1_s.at[1], c1_r, 0, 1).start()
+        assemble_panel(lambda t, i: send(
+            ar.at[i, t], ar.at[i, t], c1_s.at[1], c1_r, 0, 1
+        ).start())
         second_pivot(x3, wide, small, r_ref)
         pivots_from_root(1)
         pivots_out(1)
@@ -377,16 +383,24 @@
     @pl.when((c == 0) & (r > 0))
     def _():
         move(front.at[pl.ds(0, 4)], pf.at[pl.ds(0, 4)], 0).wait()
-        assemble_panel()
-        each(1, NC, lambda q: send(
-            ar.at[q // 2, lax.rem(q, 2)], ar.at[q // 2, lax.rem(q, 2)], c1_s.at[q], c1_r, r, q
-        ).start())
-        each(1, 8, lambda q: send(
-            ar.at[0, 0], ar.at[0, 0], c2_s.at[q], c2_r.at[0], r, 2 * q
-        ).start())
-        each(0, 8, lambda q: send(
-            ar.at[q, 0], ar.at[q, 0], c3_s.at[q], c3_r.at[q], r, 1
-        ).start())
+
+        def give_rows(t, i):
+            if t == 1:
+                send(ar.at[i, 1], ar.at[i, 1], c1_s.at[2 * i + 1], c1_r, r, 2 * i + 1).start()
+                return
+            send(ar.at[i, 0], ar.at[i, 0], c3_s.at[i], c3_r.at[i], r, 1).start()
+
+            @pl.when(i > 0)
+            def _():
+                send(ar.at[i, 0], ar.at[i, 0], c1_s.at[2 * i], c1_r, r, 2 * i).start()
+
+            @pl.when(i == 0)
+            def _():
+                each(1, 8, lambda q: send(
+                    ar.at[0, 0], ar.at[0, 0], c2_s.at[q], c2_r.at[0], r, 2 * q
+                ).start())
+
+        assemble_panel(give_rows)
         for t in range(2):
             send(part(x3, r, t), part(x3, r, t), x1_s.at[0], x1_r.at[t], 0, 0).wait_recv()
             pivots_out(t)
@@ -403,13 +417,16 @@
 
         def run(d):
             q = lax.rem(r + d, NR)
-            mine = wide_kids.at[pl.ds(8 * q + 4 * m, 4)]
-            there = kids.at[r, pl.ds(4 * m, 4)]
+            mine = held[m].at[pl.ds(8 * q, 8)]
+            there = kids.at[r, pl.ds(8 * m, 8)]
 
             @pl.when(q >= h)
             def _():
                 for n in range(4):
-                    wide_kids[8 * q + 4 * m + n] = e1r[m][tab[q] + n]
+                    for u in range(2):
+                        held[m][8 * q + 2 * n + u] = e1r[m][
+                            tab[q] + n, 128 * u : 128 * u + 128, :
+                        ]
 
                 @pl.when(q != r)
                 def _():
@@ -438,8 +455,36 @@
         def _():
             send(ar.at[q, core], ar.at[q, core], c3_s.at[q], c3_r.at[q], r, sibling).start()
 
-    @pl.when((c > 0) & (r > 0))
-    def _():
+    def match_along(ref, row, t):
+        def on(d):
+            q = 4 * z + lax.rem(y + d, 4)
+
+            @pl.when(q > h)
+            def _():
+                send(
+                    ref.at[row, t], ac.at[y, t],
+                    d2_s.at[4 * t + lax.rem(q, 4)], d2_r.at[4 * t + y], q, c,
+                ).start()
+
+        each(1, 4, on)
+
+    def match_on(ref, row, t):
+        @pl.when(z == 0)
+        def _():
+            send(ref.at[row, t], ac.at[y, t], dz_s.at[t], dz_r.at[t], partner, c).start()
+
+        match_along(ref, row, t)
+
+    def match_from(t):
+        @pl.when((r == h) & (c > 0))
+        def _():
+            each(1, 4, lambda d: send(
+                ar.at[4 * core + lax.rem(y + d, 4), t], ac.at[lax.rem(y + d, 4), t],
+                d1_s.at[4 * t + lax.rem(y + d, 4)], d1_r.at[t], 4 * z + lax.rem(y + d, 4), c,
+            ).start())
+            match_on(ar, 4 * core + y, t)
+
+    def own_half():
         send(ar.at[h, core], ar.at[h, core], c1_s.at[0], c1_r, r, 0).wait_recv()
 
         def spread(d):
@@ -462,52 +507,53 @@
             across(q)
 
         each(1, 8, collect)
+
+    def other_half():
         each(0, 8, lambda q: send(
             ar.at[q, 1 - core], ar.at[q, 1 - core], c3_s.at[q], c3_r.at[q], r, sibling
         ).wait_recv())
 
+    @pl.when((r > 0) & (c > 0) & (core == 0))
+    def _():
+        own_half()
+        match_from(0)
+        other_half()
+        match_from(1)
+
+    @pl.when((r > 0) & (core == 1))
+    def _():
+        other_half()
+        match_from(0)
+        own_half()
+        match_from(1)
+
+    @pl.when((r == 0) & (c == 1))
+    def _():
+        match_from(0)
+        match_from(1)
+
     @pl.when(c > 0)
     def _():
         @pl.when(r >= h)
         def _():
             move(ar, ar_out, 3).start()
 
-        def match_along(piece):
-            def on(d):
-                q = 4 * z + lax.rem(y + d, 4)
-
-                @pl.when(q > h)
-                def _():
-                    send(piece, ac.at[y], d2_s.at[lax.rem(q, 4)], d2_r.at[y], q, c).start()
-
-            each(1, 4, on)
-
-        def match_on(piece):
-            @pl.when(z == 0)
-            def _():
-                send(piece, ac.at[y], dz_s, dz_r, partner, c).start()
-
-            match_along(piece)
-
         @pl.when(r == h)
         def _():
             move(ar.at[pl.ds(4 * core, 4)], ac_out, 4).start()
 
-            each(1, 4, lambda d: send(
-                ar.at[4 * core + lax.rem(y + d, 4)], ac.at[lax.rem(y + d, 4)],
-                d1_s.at[lax.rem(y + d, 4)], d1_r, 4 * z + lax.rem(y + d, 4), c,
-            ).start())
-            match_on(ar.at[4 * core + y])
 
         @pl.when((r != h) & (z == h // 4))
         def _():
-            send(ac.at[y], ac.at[y], d1_s.at[0], d1_r, h, c).wait_recv()
-            match_on(ac.at[y])
+            for t in range(2):
+                send(ac.at[y, t], ac.at[y, t], d1_s.at[0], d1_r.at[t], h, c).wait_recv()
+                match_on(ac, y, t)
 
         @pl.when(z > h // 4)
         def _():
-            send(ac.at[y], ac.at[y], dz_s, dz_r, partner, c).wait_recv()
-            match_along(ac.at[y])
+            for t in range(2):
+                send(ac.at[y, t], ac.at[y, t], dz_s.at[t], dz_r.at[t], partner, c).wait_recv()
+                match_along(ac, y, t)
 
         def pivots_along(p, t, base):
             each(1, 4, lambda d: send(
@@ -530,10 +576,11 @@
 
         @pl.when(r > h)
         def _():
-            each(1, 4, lambda d: send(
-                ac.at[lax.rem(y + d, 4)], ac.at[lax.rem(y + d, 4)],
-                d2_s.at[0], d2_r.at[lax.rem(y + d, 4)], 4 * z + lax.rem(y + d, 4), c,
-            ).wait_recv())
+            for t in range(2):
+                each(1, 4, lambda d: send(
+                    ac.at[lax.rem(y + d, 4), t], ac.at[lax.rem(y + d, 4), t],
+                    d2_s.at[0], d2_r.at[4 * t + lax.rem(y + d, 4)], 4 * z + lax.rem(y + d, 4), c,
+                ).wait_recv())
             move(ac, ac_out, 4).start()
 
         @pl.when(r >= h)
@@ -543,7 +590,7 @@
                 def _():
                     for m in range(2):
                         send(
-                            wide_kids.at[pl.ds(0, 4)], kids.at[q, pl.ds(4 * m, 4)],
+                            held[m].at[pl.ds(0, 8)], kids.at[q, pl.ds(8 * m, 8)],
                             e2_s.at[0], e2_r.at[8 * m + q], q, c,
                         ).wait_recv()
 
@@ -579,9 +626,10 @@
     @pl.when(c < 2)
     def _():
         unless(root, lambda: sent(turned.at[pl.ds(0, 2)], k_s))
-        each(0, NR, lambda q: when(
-            (q != r) | (c == 1), lambda: sent(bs.at[q], b_s.at[q])
-        ))
+        for t in range(2):
+            each(0, NR, lambda q: when(
+                (q != r) | (c == 1), lambda: sent(bs.at[t, q], b_s.at[8 * t + q])
+            ))
 
     when(c == 0, lambda: left_col(0))
     left_col(1)
@@ -613,9 +661,9 @@
     def _():
         def left_row(q):
             for m in range(2):
-                mine = wide_kids.at[pl.ds(8 * q + 4 * m, 4)]
+                mine = held[m].at[pl.ds(8 * q, 8)]
                 when(q != r, lambda: sent(mine, e2_s.at[8 * m + q]))
-                when(q == r, lambda: move(mine, kids.at[r, pl.ds(4 * m, 4)], 5 + m).wait())
+                when(q == r, lambda: move(mine, kids.at[r, pl.ds(8 * m, 8)], 5 + m).wait())
 
         each(h, NR, left_row)
 
@@ -639,14 +687,19 @@
             move(ar, ar_out, 3).wait()
             move(ac, ac_out, 4).wait()
 
-        when(r == h, lambda: each(1, 4, lambda d: sent(ac.at[0], d1_s.at[lax.rem(y + d, 4)])))
+        for t in range(2):
+            when(r == h, lambda: each(1, 4, lambda d: sent(
+                ac.at[0, 0], d1_s.at[4 * t + lax.rem(y + d, 4)]
+            )))
 
         @pl.when(z >= h // 4)
         def _():
-            when((z == 0) & (h < 4), lambda: sent(ac.at[0], dz_s))
-            each(1, 4, lambda d: when(
-                4 * z + lax.rem(y + d, 4) > h, lambda: sent(ac.at[0], d2_s.at[lax.rem(y + d, 4)])
-            ))
+            for t in range(2):
+                when((z == 0) & (h < 4), lambda: sent(ac.at[0, 0], dz_s.at[t]))
+                each(1, 4, lambda d: when(
+                    4 * z + lax.rem(y + d, 4) > h,
+                    lambda: sent(ac.at[0, 0], d2_s.at[4 * t + lax.rem(y + d, 4)]),
+                ))
 
 
 def exchange(tab, fm, child, front):
@@ -657,7 +710,7 @@
         in_specs=[SM, SM, VM, ANY],
         out_specs=[ANY] * 6,
         out_shape=[
-            sds((NR, 8, BS, BS), bf16),
+            sds((NR, 16, 128, BS), bf16),
             sds((8, 2, 128, 1024), bf16),
             sds((4, 2, 128, 1024), bf16),
             sds((8, 3, 64, 512), bf16),
@@ -671,8 +724,9 @@
             pltpu.VMEM((NC, 2, BS, BS), bf16),
             pltpu.VMEM((NC, BS, BS), bf16),
             pltpu.VMEM((NC, BS, BS), bf16),
-            pltpu.VMEM((64, BS, BS), bf16),
-            pltpu.VMEM((NR, 4, BS, BS), bf16),
+            pltpu.VMEM((64, 128, BS), bf16),
+            pltpu.VMEM((64, 128, BS), bf16),
+            pltpu.VMEM((2, NR, 4, 128, BS), bf16),
             pltpu.VMEM((8, BS, 1024), f32),
             pltpu.VMEM((8, 2, 128, 1024), bf16),
             pltpu.VMEM((4, 2, 128, 1024), bf16),
@@ -683,9 +737,9 @@
             pltpu.VMEM((128, 1536), f32),
             dma, dma((16,)),
             dma((32,)), dma((32,)), dma((16,)), dma((16,)),
-            dma((NR,)), dma((16,)),
+            dma((16,)), dma((32,)),
             dma((NC,)), dma, dma((8,)), dma((8,)), dma((8,)), dma((8,)),
-            dma((4,)), dma, dma((4,)), dma((4,)), dma, dma,
+            dma((8,)), dma((2,)), dma((8,)), dma((8,)), dma((2,)), dma((2,)),
             dma((16,)), dma((2,)), dma((32,)), dma((2,)), dma((24,)), dma((16,)), dma((7,)),
         ],
         compiler_params=pltpu.CompilerParams(
@@ -792,7 +846,11 @@
 
                     @pl.when(tab[120 + 8 * k + i] * tab[184 + 4 * k + j] > 0)
                     def _():
-                        out[:, at] = out[:, at] + times * kids[k, 4 * side + slot].astype(f32)
+                        for u in range(2):
+                            half = pl.ds(128 * u, 128)
+                            out[half, at] = out[half, at] + times * kids[
+                                k, 8 * side + 2 * slot + u
+                            ].astype(f32)
 
             @pl.when(jnp.logical_not(keep))
             def _():
@@ -814,7 +872,7 @@
             whole((4, 2, 128, 1024)),
             whole((8, 3, 64, 512)),
             whole((8, 3, 64, 512)),
-            whole((NR, 8, BS, BS)),
+            whole((NR, 16, 128, BS)),
         ],
         out_specs=pl.BlockSpec((BS, 1024), lambda i: (i, 0)),
         out_shape=jax.ShapeDtypeStruct((2048, 1024), f32),

time: 293 us -> 278 us (0.949)
  the two profiles are of different devices: /device:TPU:112 before, /device:TPU:38 now
where the time goes in v4:
time: 278 us; the launch traced here: 277 us
  Pallas kernels  269 us (97%)
  local copies, waits for them, and re-layouts  4.83 us (2%)
  other arithmetic  3.16 us (1%)
    pallas_call x1, Pallas kernels, exchange(): pl.pallas_call(exchange_kernel, in_specs=[SM, SM, VM, ANY], out_specs=[AN...  245 us
    pallas_call x1, Pallas kernels, update(): pl.pallas_call(update_kernel, grid=(8,), in_specs=[SM, SM, pl.BlockSpec((...  24.4 us

profile of v4, /device:TPU:38, one launch (start us, length us, event | category | flops | bytes accessed | tf_op | source)
XLA Modules:
  0.0 277.3 jit_solution(8880977496880156421)
XLA Ops:
  0.0 0.7 dynamic-slice_bitcast_fusion
  0.7 0.8 convert_reduce_fusion.1
  1.6 0.2 convert_reduce_fusion.3
  1.8 0.1 convert_reduce_fusion
  1.8 0.1 subtract_add_fusion
  1.9 0.9 select_reduce_fusion.1
  2.8 0.1 copy.5
  2.9 0.1 max.17
  3.0 0.1 copy.6
  3.1 0.1 reshape.104
  3.2 0.1 subtract_add_fusion.1
  3.2 1.0 select_reduce_fusion
  4.2 0.1 reshape.103
  4.3 0.1 max.15
  4.4 0.7 concatenate.3.tab
  5.1 0.0 copy-start.2
  5.1 0.0 copy-start.3
  5.1 244.8 %exchange.1 = (bf16[8,16,128,256]{3,2,1,0:T(8,128)(2,1)}, bf16[8,2,128,1024]{3,2,1,0:T(8,128)(2,1)}, bf16[4,2,128,1024]{3,2,1,0:T(8,128)(2,1)}, bf16[8,3,64,512]...) custom-call(s32[216]{0:T(256)} %concatenate.3.tab, s32[64,64]{1,0:T(8,128)} %fm.3, ...), custom_call_target="tpu_custom_call" | custom-call | bytes 400000000 | tf_op jit(solution)/shard_map/exchange/pallas_call | solution.py:708
  249.9 0.0 copy-done.2
  249.9 0.0 copy-done.3
  249.9 0.0 copy-start
  249.9 1.6 copy-done
  251.5 0.0 copy-start.1
  251.5 1.4 copy-done.1
  252.9 24.4 %update.1 = f32[2048,1024]{1,0:T(8,128)} custom-call(s32[216]{0:T(256)S(1)} %copy-done.3, s32[64,64]{1,0:T(8,128)S(1)} %copy-done.2, f32[2048,1024]{1,0:T(8,128)} %front.1, f32[8,256,1024]{2,1,0:T(8,128)} %get-tuple-element.11.panel, bf16[8,2,128,1024]{3,2,1,0:T(8,128)(2,1)} %get-tuple-element.12.ar, bf16[4,2,128,1024]{3,2,1,0:T(8,128)(2,1)S(1)} %copy-done, ...), custom_call_target="tpu_custom_call" | custom-call | tf_op jit(solution)/shard_map/update/pallas_call | solution.py:864
  (11 shorter events, 0.1 us)
Async XLA Ops:
  5.1 244.8 %copy-start.2 = (s32[64,64]{1,0:T(8,128)S(1)}, s32[64,64]{1,0:T(8,128)}, u32[]{:S(2)}) copy-start(s32[64,64]{1,0:T(8,128)} %fm.3) | copy-start | bytes 49156
  5.1 244.9 %copy-start.3 = (s32[216]{0:T(256)S(1)}, s32[216]{0:T(256)}, u32[]{:S(2)}) copy-start(s32[216]{0:T(256)} %concatenate.3.tab) | copy-start | bytes 2596
  249.9 1.6 copy-start
  251.5 1.4 copy-start.1

commit v5 on v4

--- a/solution.py
+++ b/solution.py
@@ -396,7 +396,7 @@
 
             @pl.when(i == 0)
             def _():
-                each(1, 8, lambda q: send(
+                each(1, r + 1, lambda q: send(
                     ar.at[0, 0], ar.at[0, 0], c2_s.at[q], c2_r.at[0], r, 2 * q
                 ).start())
 
@@ -451,7 +451,7 @@
         send(ar, ar, c1_s.at[0], c1_r, 0, 0).wait_recv()
 
     def across(q):
-        @pl.when(c != 1)
+        @pl.when((c != 1) & (h <= r))
         def _():
             send(ar.at[q, core], ar.at[q, core], c3_s.at[q], c3_r.at[q], r, sibling).start()
 
@@ -490,7 +490,7 @@
         def spread(d):
             q = lax.rem(h + d, 8)
 
-            @pl.when((q != 0) | (core != 0))
+            @pl.when((q <= r) & ((q != 0) | (core != 0)))
             def _():
                 send(
                     ar.at[h, core], ar.at[h, core], c2_s.at[q], c2_r.at[h], r, 2 * q + core
@@ -506,12 +506,12 @@
             ).wait_recv()
             across(q)
 
-        each(1, 8, collect)
+        when(h <= r, lambda: each(1, 8, collect))
 
     def other_half():
-        each(0, 8, lambda q: send(
+        when(h <= r, lambda: each(0, 8, lambda q: send(
             ar.at[q, 1 - core], ar.at[q, 1 - core], c3_s.at[q], c3_r.at[q], r, sibling
-        ).wait_recv())
+        ).wait_recv()))
 
     @pl.when((r > 0) & (c > 0) & (core == 0))
     def _():
@@ -648,7 +648,7 @@
         @pl.when(r > 0)
         def _():
             each(1, NC, lambda q: sent(ar.at[0, 0], c1_s.at[q]))
-            each(1, 8, lambda q: sent(ar.at[0, 0], c2_s.at[q]))
+            each(1, r + 1, lambda q: sent(ar.at[0, 0], c2_s.at[q]))
             each(0, 8, lambda q: sent(ar.at[q, 0], c3_s.at[q]))
 
         for t in range(2):
@@ -669,10 +669,13 @@
 
         @pl.when(r > 0)
         def _():
-            each(0, 8, lambda q: when(
+            each(0, r + 1, lambda q: when(
                 (q != h) & ((q != 0) | (core != 0)), lambda: sent(ar.at[0, 0], c2_s.at[q])
             ))
-            when(c != 1, lambda: each(0, 8, lambda q: sent(ar.at[0, 0], c3_s.at[q])))
+            when(
+                (c != 1) & (h <= r),
+                lambda: each(0, 8, lambda q: sent(ar.at[0, 0], c3_s.at[q])),
+            )
 
         for t in range(2):
             sent(part(xb, 0, t), x3_s.at[12 * t + partner])
@@ -756,7 +759,8 @@
 
 
 def update_kernel(
-    tab, fm, front, panel, ar, ac, xb, x3, kids, out, inv0, low, inv1, low0, low1, low2, wc,
+    tab, fm, front, panel, ar, ac, xb, x3, kids_in, out,
+    inv0, low, inv1, low0, low1, low2, wc, kids, came,
 ):
     r = lax.axis_index("row")
     c = lax.axis_index("col")
@@ -788,6 +792,8 @@
 
     @pl.when((i == 0) & (c > 0) & (c // 2 <= r))
     def _():
+        fetch = pltpu.make_async_copy(kids_in, kids, came)
+        fetch.start()
         inv0[...] = gather(xb, 0)
         low[...] = gather(xb, 1)
         inv1[...] = gather(xb, 2)
@@ -796,6 +802,7 @@
             first, second = solve(block[:, :512], block[:, 512:], 4 * c + j)
             wc[BS * j : BS * j + BS, :512] = first
             wc[BS * j : BS * j + BS, 512:] = second
+        fetch.wait()
 
     @pl.when((i == 0) & (c == 0))
     def _():
@@ -872,11 +879,16 @@
             whole((4, 2, 128, 1024)),
             whole((8, 3, 64, 512)),
             whole((8, 3, 64, 512)),
-            whole((NR, 16, 128, BS)),
+            ANY,
         ],
         out_specs=pl.BlockSpec((BS, 1024), lambda i: (i, 0)),
         out_shape=jax.ShapeDtypeStruct((2048, 1024), f32),
-        scratch_shapes=[pltpu.VMEM((512, 512), bf16)] * 6 + [pltpu.VMEM((1024, 1024), bf16)],
+        scratch_shapes=[pltpu.VMEM((512, 512), bf16)] * 6
+        + [
+            pltpu.VMEM((1024, 1024), bf16),
+            pltpu.VMEM((NR, 16, 128, BS), bf16),
+            pltpu.SemaphoreType.DMA,
+        ],
         compiler_params=pltpu.CompilerParams(vmem_limit_bytes=48 << 20),
         name="update",
     )(tab, fm, front, panel, ar, ac, xb, x3, kids)

time: 278 us -> 273 us (0.982)
  the two profiles are of different devices: /device:TPU:38 before, /device:TPU:112 now
where the time goes in v5:
time: 273 us; the launch traced here: 269 us
  Pallas kernels  261 us (96%)
  local copies, waits for them, and re-layouts  4.83 us (2%)
  other arithmetic  3.16 us (1%)
    pallas_call x1, Pallas kernels, exchange(): pl.pallas_call(exchange_kernel, in_specs=[SM, SM, VM, ANY], out_specs=[AN...  237 us
    pallas_call x1, Pallas kernels, update(): pl.pallas_call(update_kernel, grid=(8,), in_specs=[SM, SM, pl.BlockSpec((...  23.3 us

profile of v5, /device:TPU:112, one launch (start us, length us, event | category | flops | bytes accessed | tf_op | source)
XLA Modules:
  0.0 268.9 jit_solution(1054764654954075310)
XLA Ops:
  0.0 0.7 dynamic-slice_bitcast_fusion
  0.7 0.8 convert_reduce_fusion.1
  1.6 0.2 convert_reduce_fusion.3
  1.8 0.1 convert_reduce_fusion
  1.8 0.1 subtract_add_fusion
  1.9 0.9 select_reduce_fusion.1
  2.8 0.1 copy.5
  2.9 0.1 max.17
  3.0 0.1 copy.6
  3.1 0.1 reshape.104
  3.2 0.1 subtract_add_fusion.1
  3.2 1.0 select_reduce_fusion
  4.2 0.1 reshape.103
  4.3 0.1 max.15
  4.4 0.7 concatenate.3.tab
  5.1 0.0 copy-start.2
  5.1 0.0 copy-start.3
  5.1 237.4 %exchange.1 = (bf16[8,16,128,256]{3,2,1,0:T(8,128)(2,1)}, bf16[8,2,128,1024]{3,2,1,0:T(8,128)(2,1)}, bf16[4,2,128,1024]{3,2,1,0:T(8,128)(2,1)}, bf16[8,3,64,512]...) custom-call(s32[216]{0:T(256)} %concatenate.3.tab, s32[64,64]{1,0:T(8,128)} %fm.3, ...), custom_call_target="tpu_custom_call" | custom-call | bytes 400000000 | tf_op jit(solution)/shard_map/exchange/pallas_call | solution.py:711
  242.4 0.0 copy-done.2
  242.4 0.0 copy-done.3
  242.5 0.0 copy-start
  242.5 1.6 copy-done
  244.0 0.0 copy-start.1
  244.0 1.4 copy-done.1
  245.5 23.3 %update.1 = f32[2048,1024]{1,0:T(8,128)} custom-call(s32[216]{0:T(256)S(1)} %copy-done.3, s32[64,64]{1,0:T(8,128)S(1)} %copy-done.2, f32[2048,1024]{1,0:T(8,128)} %front.1, f32[8,256,1024]{2,1,0:T(8,128)} %get-tuple-element.11.panel, bf16[8,2,128,1024]{3,2,1,0:T(8,128)(2,1)} %get-tuple-element.12.ar, bf16[4,2,128,1024]{3,2,1,0:T(8,128)(2,1)S(1)} %copy-done, ...), custom_call_target="tpu_custom_call" | custom-call | tf_op jit(solution)/shard_map/update/pallas_call | solution.py:871
  (11 shorter events, 0.1 us)
Async XLA Ops:
  5.1 237.4 %copy-start.2 = (s32[64,64]{1,0:T(8,128)S(1)}, s32[64,64]{1,0:T(8,128)}, u32[]{:S(2)}) copy-start(s32[64,64]{1,0:T(8,128)} %fm.3) | copy-start | bytes 49156
  5.1 237.4 %copy-start.3 = (s32[216]{0:T(256)S(1)}, s32[216]{0:T(256)}, u32[]{:S(2)}) copy-start(s32[216]{0:T(256)} %concatenate.3.tab) | copy-start | bytes 2596
  242.5 1.6 copy-start
  244.0 1.4 copy-start.1

commit v6 on v5

--- a/solution.py
+++ b/solution.py
@@ -2,6 +2,7 @@
 
 import jax
 import jax.numpy as jnp
+import numpy as np
 from jax import lax
 from jax.experimental import pallas as pl
 from jax.experimental.pallas import tpu as pltpu
@@ -895,25 +896,31 @@
 
 
 def tables(maps, r, c):
-    own = lax.dynamic_index_in_dim(maps, r, 0, keepdims=False)
-    row_start = jnp.minimum(jnp.sum(own[:, None] < 8 * jnp.arange(NR), axis=0), 12)
-    col_start = jnp.minimum(jnp.sum(own[:, None] < 4 * jnp.arange(NC), axis=0), 14)
-    index = jnp.arange(16)
-    rows = maps[:, None, :] == 8 * r + jnp.arange(8)[None, :, None]
-    row_first = jnp.minimum(jnp.sum(maps < 8 * r, axis=1), 12)
-    row_slot = jnp.sum(rows * (index - row_first[:, None, None] + 1), axis=-1) - 1
-    cols = maps[:, None, :] == 4 * c + jnp.arange(4)[None, :, None]
-    col_first = jnp.minimum(jnp.sum(maps < 4 * c, axis=1), 14)
-    col_slot = jnp.sum(cols * (index - col_first[:, None, None] + 1), axis=-1) - 1
-    parts = [
-        row_start,
-        col_start,
-        jnp.maximum(row_slot, 0).reshape(-1),
-        jnp.maximum(col_slot, 0).reshape(-1),
-        (row_slot >= 0).reshape(-1),
-        (col_slot >= 0).reshape(-1),
-    ]
-    return jnp.concatenate([part.astype(jnp.int32) for part in parts])
+    q8, q16 = np.arange(NR), np.arange(NC)
+    kr, ir = np.repeat(q8, 8), np.tile(q8, 8)
+    kc, jc = np.repeat(q8, 4), np.tile(np.arange(4), 8)
+    nothing = np.zeros(24, np.int32)
+    join = lambda *parts: np.concatenate(parts).astype(np.int32)
+    own = join(nothing + 1, 0 * kr, 0 * kc, 0 * kr, 0 * kc)
+    child = join(nothing, kr, kc, kr, kc)
+    per_row = join(nothing, 8 + 0 * kr, 0 * kc, 8 + 0 * kr, 0 * kc)
+    per_col = join(nothing, 0 * kr, 4 + 0 * kc, 0 * kr, 4 + 0 * kc)
+    start = join(8 * q8, 4 * q16, 0 * kr, 0 * kc, 0 * kr, 0 * kc)
+    block = join(nothing, ir, jc, ir, jc)
+    cap = join(12 + 0 * q8, 14 + 0 * q16, 12 + 0 * kr, 14 + 0 * kc, 0 * kr, 0 * kc)
+    base = start + per_row * r + per_col * c
+    mine = jnp.where(own == 1, r, child)[:, None, None] == jnp.arange(NR)[:, None]
+    below = jnp.sum(mine & (maps < base[:, None, None]), axis=(1, 2), dtype=jnp.int32)
+    found = jnp.sum(
+        (mine & (maps == (base + block)[:, None, None])) * jnp.arange(1, 17, dtype=jnp.int32),
+        axis=(1, 2), dtype=jnp.int32,
+    )
+    first = jnp.minimum(below, cap)
+    return jnp.where(
+        own == 1,
+        first,
+        jnp.where(cap == 0, (found > 0).astype(jnp.int32), jnp.where(found > 0, found - 1 - first, 0)),
+    )
 
 
 def local(front, child_updates, child_maps, fill_mask):

time: 273 us -> 271 us (level)
  no operation moved by 1% of the time
where the time goes in v6:
time: 271 us; the launch traced here: 267 us
  Pallas kernels  261 us (96%)
  local copies, waits for them, and re-layouts  3 us (1%)
  other arithmetic  2.87 us (1%)
    pallas_call x1, Pallas kernels, exchange(): pl.pallas_call(exchange_kernel, in_specs=[SM, SM, VM, ANY], out_specs=[AN...  237 us
    pallas_call x1, Pallas kernels, update(): pl.pallas_call(update_kernel, grid=(8,), in_specs=[SM, SM, pl.BlockSpec((...  23.4 us

profile of v6, /device:TPU:112, one launch (start us, length us, event | category | flops | bytes accessed | tf_op | source)
XLA Modules:
  0.0 266.8 jit_solution(16136727283795451316)
XLA Ops:
  0.0 0.8 fusion
  0.8 0.8 convert_reduce_fusion
  1.6 1.3 select_select_fusion.tab
  2.9 0.0 copy-start.2
  2.9 0.0 copy-start.3
  2.9 237.4 %exchange.1 = (bf16[8,16,128,256]{3,2,1,0:T(8,128)(2,1)}, bf16[8,2,128,1024]{3,2,1,0:T(8,128)(2,1)}, bf16[4,2,128,1024]{3,2,1,0:T(8,128)(2,1)}, bf16[8,3,64,512]...) custom-call(s32[216]{0:T(256)} %select_select_fusion.tab, s32[64,64]{1,0:T(8,128)} %fm.3, ...), custom_call_target="tpu_custom_call" | custom-call | bytes 400000000 | tf_op jit(solution)/shard_map/exchange/pallas_call | solution.py:712
  240.3 0.0 copy-done.2
  240.3 0.0 copy-done.3
  240.3 0.0 copy-start
  240.3 1.6 copy-done
  241.9 0.0 copy-start.1
  241.9 1.4 copy-done.1
  243.3 23.4 %update.1 = f32[2048,1024]{1,0:T(8,128)} custom-call(s32[216]{0:T(256)S(1)} %copy-done.3, s32[64,64]{1,0:T(8,128)S(1)} %copy-done.2, f32[2048,1024]{1,0:T(8,128)} %front.1, f32[8,256,1024]{2,1,0:T(8,128)} %get-tuple-element.11.panel, bf16[8,2,128,1024]{3,2,1,0:T(8,128)(2,1)} %get-tuple-element.12.ar, bf16[4,2,128,1024]{3,2,1,0:T(8,128)(2,1)S(1)} %copy-done, ...), custom_call_target="tpu_custom_call" | custom-call | tf_op jit(solution)/shard_map/update/pallas_call | solution.py:872
  (2 shorter events, 0.0 us)
Async XLA Ops:
  2.9 237.4 %copy-start.2 = (s32[64,64]{1,0:T(8,128)S(1)}, s32[64,64]{1,0:T(8,128)}, u32[]{:S(2)}) copy-start(s32[64,64]{1,0:T(8,128)} %fm.3) | copy-start | bytes 49156
  2.9 237.4 %copy-start.3 = (s32[216]{0:T(256)S(1)}, s32[216]{0:T(256)}, u32[]{:S(2)}) copy-start(s32[216]{0:T(256)} %select_select_fusion.tab) | copy-start | bytes 2596
  240.3 1.6 copy-start
  241.9 1.4 copy-start.1
